TPU v7x, 256 devices: a whole 4x4x8 slice. The times are simulated.
256 devices in a mesh: rows: 8 (over x, core), vocab: 32 (over z, y).
Axes of the slice: x: 4, y: 4, z: 8, core: 2. Of those that a mesh axis runs over, the one named last changes fastest.
Arguments:
- draft_hidden: bfloat16 [4096, 2048], P('rows'), may hold values from -128 to 128
- teacher_hidden: bfloat16 [4096, 8192], P('rows'), may hold values from -128 to 128
- draft_head: bfloat16 [2048, 32768], P(None, 'vocab'), may hold values from -4 to 4
- teacher_head: bfloat16 [8192, 32768], P(None, ('vocab', 'rows')), may hold values from -4 to 4
- row_weight: float32 [4096], P('rows'), may hold values from 1 to 16
Outputs:
- grad_hidden: bfloat16 [4096, 2048], P('rows')
- grad_head: bfloat16 [2048, 32768], P('rows', 'vocab')
- kl_rows: float32 [4096], P('rows')
All inputs are finite; a program needn't handle non-finite values.
Results may differ from a plain program's by a relative error of at most 0.0051.
Values may be sent and summed in bfloat16 or wider, within the bound.
No kernel may reach another device: no remote copies, remote signals or barrier semaphores. Data moves between devices by JAX's collectives and lax.ppermute only.
A program may use at most 192 MiB of HBM per device.

v0:
```python
import jax
import jax.numpy as jnp
from jax import lax
from jax.sharding import Mesh
from jax.sharding import PartitionSpec as P


ROWS = ("x", "core")
VOCAB = ("z", "y")
VOCAB_ROWS = ("z", "y", "x", "core")


def shifted(x, axis, by):
    n = lax.axis_size(axis)
    return lax.ppermute(x, axis, [(i, (i + by) % n) for i in range(n)])


def dot(a, b, contract):
    return lax.dot_general(a, b, (contract, ((), ())), preferred_element_type=jnp.float32)


def exchanged(pieces, axis):
    return lax.all_to_all(pieces, axis, 0, 0, tiled=True)


def sent_to_all(x, axis):
    return exchanged(jnp.broadcast_to(x[None], (lax.axis_size(axis), *x.shape)), axis)


def combined(pieces):
    draft_top = jnp.max(pieces[:, 0], axis=0)
    teach_top = jnp.max(pieces[:, 2], axis=0)
    draft_scale = jnp.exp(pieces[:, 0] - draft_top)
    teach_scale = jnp.exp(pieces[:, 2] - teach_top)
    return jnp.stack(
        [
            draft_top,
            jnp.sum(pieces[:, 1] * draft_scale, axis=0),
            teach_top,
            jnp.sum(pieces[:, 3] * teach_scale, axis=0),
            jnp.sum(pieces[:, 4] * teach_scale, axis=0),
        ]
    )


def teacher_product(hidden, own):
    place, core = lax.axis_index("x"), lax.axis_index("core")
    ring = lax.axis_size("x")

    def turned(piece, way):
        pairs = [
            (2 * i + c, 2 * ((i + (way if c == 0 else -way)) % ring) + c)
            for i in range(ring)
            for c in range(2)
        ]
        return lax.ppermute(piece, ROWS, pairs)

    def product(mine, others):
        pair = jnp.where(
            core == 0,
            jnp.concatenate([mine, others], axis=1),
            jnp.concatenate([others, mine], axis=1),
        )
        return dot(hidden, pair, ((1,), (0,)))

    behind, ahead = turned(own, 1), turned(own, -1)
    far = turned(behind, 1)
    own_part = product(own, shifted(own, "core", 1))
    behind_part = product(behind, shifted(ahead, "core", 1))
    ahead_part = product(ahead, shifted(behind, "core", 1))
    far_part = product(far, shifted(far, "core", 1))
    width = 2 * own.shape[1]
    back = jnp.where(core == 0, ring - 1, 1)
    logits = jnp.zeros((hidden.shape[0], ring * width), jnp.float32)
    for step, part in ((0, own_part), (back, behind_part), (ring - back, ahead_part), (2, far_part)):
        at = (place + step) % ring
        logits = lax.dynamic_update_slice(logits, part, (0, at * width))
    return logits


def swapped(pieces, axis):
    n, place = lax.axis_size(axis), lax.axis_index(axis)
    found = []
    for by in range(n):
        piece = lax.dynamic_index_in_dim(pieces, (place + by) % n, 0, keepdims=False)
        found.append(shifted(piece, axis, by) if by else piece)
    return found


def gathered(block, axis):
    n, place = lax.axis_size(axis), lax.axis_index(axis)
    whole = jnp.zeros((n, *block.shape), block.dtype)
    for by in range(n):
        piece = shifted(block, axis, by) if by else block
        whole = lax.dynamic_update_index_in_dim(whole, piece, (place - by) % n, 0)
    return whole


def added(pieces):
    return sum(piece.astype(jnp.float32) for piece in pieces).astype(jnp.bfloat16)


def summed_head(draft_hidden, grad_logits):
    core = lax.axis_index("core")
    tokens, width = draft_hidden.shape
    ring = lax.axis_size("x")
    strips = draft_hidden.reshape(tokens, ring, 2, width // (2 * ring))

    def strip(which):
        return lax.dynamic_index_in_dim(strips, which, 2, keepdims=False).reshape(tokens, width // 2)

    away = dot(strip(1 - core), grad_logits, ((0,), (0,))).astype(jnp.bfloat16)
    away = shifted(away, "core", 1)
    mine = dot(strip(core), grad_logits, ((0,), (0,)))
    pair = (mine + away.astype(jnp.float32)).astype(jnp.bfloat16)
    pieces = swapped(pair.reshape(ring, -1, pair.shape[1]), "x")
    return added(pieces)


def summed(part):
    n, m = lax.axis_size("y"), lax.axis_size("z")
    pieces = swapped(part.reshape(n, -1, part.shape[1]), "y")
    rows = added(pieces)
    pieces = exchanged(rows.reshape(m, -1, rows.shape[1]), "z")
    block = added(pieces)
    rows = sent_to_all(block, "z").reshape(rows.shape)
    return gathered(rows, "y").reshape(part.shape)


def stage(draft_hidden, teacher_hidden, draft_head, teacher_head, row_weight):
    draft_logits = dot(draft_hidden, draft_head, ((1,), (0,)))
    local_draft = jnp.max(draft_logits, axis=1)
    teacher_logits = teacher_product(teacher_hidden, teacher_head)
    local_teach = jnp.max(teacher_logits, axis=1)
    teach_exp = jnp.exp(teacher_logits - local_teach[:, None])
    stats = jnp.stack(
        [
            local_draft,
            jnp.sum(jnp.exp(draft_logits - local_draft[:, None]), axis=1),
            local_teach,
            jnp.sum(teach_exp, axis=1),
            jnp.sum(teach_exp * (teacher_logits - draft_logits), axis=1),
        ]
    )
    stats = combined(sent_to_all(stats, "y"))
    draft_top, draft_sum, teach_top, teach_sum, teach_gap = combined(sent_to_all(stats, "z"))
    draft_lse = draft_top + jnp.log(draft_sum)
    teacher_lse = teach_top + jnp.log(teach_sum)
    kl_rows = row_weight * (teach_gap / teach_sum - teacher_lse + draft_lse)
    teacher_prob = jnp.exp(teacher_logits - teacher_lse[:, None])
    draft_prob = jnp.exp(draft_logits - draft_lse[:, None])
    grad_logits = (row_weight[:, None] * (draft_prob - teacher_prob)).astype(jnp.bfloat16)
    grad_head = summed_head(draft_hidden, grad_logits)
    hidden_part = dot(grad_logits, draft_head, ((1,), (1,))).astype(jnp.bfloat16)
    grad_hidden = summed(hidden_part)
    return (grad_hidden, grad_head, kl_rows)


def solution(mesh):
    finer = Mesh(mesh.devices.reshape(4, 2, 8, 4), ("x", "core", "z", "y"))
    return jax.shard_map(
        stage,
        mesh=finer,
        in_specs=(P(ROWS, None), P(ROWS, None), P(None, VOCAB), P(None, VOCAB_ROWS), P(ROWS)),
        out_specs=(P(ROWS, None), P(ROWS, VOCAB), P(ROWS)),
        check_vma=False,
    )
```

profile of v0, /device:TPU:2, one launch (start us, length us, event | category | flops | bytes accessed | tf_op | source)
XLA Modules:
  0.0 219.5 jit_solution(13545237528263617479)
XLA Ops:
  0.6 2.3 %collective-permute-start.2 = (bf16[8192,128]{1,0:T(8,128)(2,1)}, bf16[8192,128]{1,0:T(8,128)(2,1)}, u32[]{:S(2)}, u32[]{:S(2)}) collective-permute-start(bf16[8192,128]{1,0:T(8,128)(2,1)} %param.8), channel_id=1, source_target_pairs={{0,192},{32,96},{64,0},{96,160},{128,64},{160,224},{192,128},{224,... | collective-permute-start | bytes 6291464 | tf_op jit(solution)/shard_map/ppermute | solution.py:56
  3.0 46.5 %collective-permute-done.2 = bf16[8192,128]{1,0:T(8,128)(2,1)} collective-permute-done((bf16[8192,128]{1,0:T(8,128)(2,1)}, bf16[8192,128]{1,0:T(8,128)(2,1)}, u32[]{:S(2)}, u32[]{:S(2)}) %collective-permute-start.2) | collective-permute-done | bytes 2097184 | tf_op jit(solution)/shard_map/ppermute | solution.py:56
  49.5 0.0 collective-permute-start.3
  49.5 0.0 collective-permute-done.1
  49.5 1.4 collective-permute-start.5
  50.8 6.6 %fusion.66 = (f32[512]{0:T(512)S(1)}, f32[512,1024]{1,0:T(8,128)}) fusion(bf16[512,2048]{1,0:T(8,128)(2,1)} %param.5, bf16[2048,1024]{1,0:T(8,128)(2,1)} %param.7), kind=kOutput, calls=%fused_computation.107 | convolution fusion | flops 2148007424 | bytes 8390656 | tf_op jit(solution)/shard_map/dot_general | solution.py:19
  57.4 0.2 broadcast_in_dim.49
  57.7 1.3 copy-done.6
  59.0 4.7 %fusion.36 = f32[512,1024]{1,0:T(8,128)S(1)} fusion(f32[512,1024]{1,0:T(8,128)S(1)} %broadcast_in_dim.49, s32[]{:T(128)S(6)} %select_n.144, bf16[512,8192]{1,0:T(8,128)(2,1)S(1)} %copy-done.4, bf16[8192,128]{1,0:T(8,128)(2,1)} %collective-permute-done, bf16[8192,128]{1,0:T(8,128)(2,1)S(1)} %copy-done.6, pred[]{:T(512)S(6)} %eq.24), kind=kOutput, calls=%fused_computation.47 | convolution fusion | flops 2166358016 | bytes 13107205 | tf_op jit(solution)/shard_map/dot_general | solution.py:19
  63.7 12.0 %collective-permute-done.5 = bf16[8192,128]{1,0:T(8,128)(2,1)S(1)} collective-permute-done((bf16[8192,128]{1,0:T(8,128)(2,1)}, bf16[8192,128]{1,0:T(8,128)(2,1)S(1)}, u32[]{:S(2)}, u32[]{:S(2)}) %collective-permute-start.5) | collective-permute-done | bytes 2097184 | tf_op jit(solution)/shard_map/ppermute | solution.py:56
  75.7 0.0 collective-permute-start.6
  75.7 0.0 collective-permute-done.3
  75.7 4.7 %fusion.34 = f32[512,1024]{1,0:T(8,128)S(1)} fusion(f32[512,1024]{1,0:T(8,128)S(1)} %fusion.36, s32[]{:T(128)S(6)} %select_n.148, bf16[512,8192]{1,0:T(8,128)(2,1)S(1)} %copy-done.4, bf16[8192,128]{1,0:T(8,128)(2,1)S(1)} %collective-permute-done.3, bf16[8192,128]{1,0:T(8,128)(2,1)} %collective-permute-done.1, pred[]{:T(512)S(6)} %eq.24), kind=kOutput, calls=%fused_computation.45 | convolution fusion | flops 2166358016 | bytes 13107205 | tf_op jit(solution)/shard_map/dot_general | solution.py:19
  80.4 0.0 collective-permute-done.4
  80.4 4.7 %fusion.32 = f32[512,1024]{1,0:T(8,128)S(1)} fusion(f32[512,1024]{1,0:T(8,128)S(1)} %fusion.34, s32[]{:T(128)S(6)} %select_n.151, bf16[512,8192]{1,0:T(8,128)(2,1)S(1)} %copy-done.4, bf16[8192,128]{1,0:T(8,128)(2,1)S(1)} %collective-permute-done.4, bf16[8192,128]{1,0:T(8,128)(2,1)} %collective-permute-done.2, pred[]{:T(512)S(6)} %eq.24), kind=kOutput, calls=%fused_computation.43 | convolution fusion | flops 2166358016 | bytes 13107205 | tf_op jit(solution)/shard_map/dot_general | solution.py:19
  85.1 0.0 collective-permute-done.6
  85.1 2.4 %fusion.30 = f32[512,1024]{1,0:T(8,128)S(1)} fusion(f32[512,1024]{1,0:T(8,128)S(1)} %fusion.32, s32[]{:T(128)S(6)} %select_n.154, bf16[512,8192]{1,0:T(8,128)(2,1)S(1)} %copy-done.4, bf16[8192,128]{1,0:T(8,128)(2,1)S(1)} %collective-permute-done.6, bf16[8192,128]{1,0:T(8,128)(2,1)S(1)} %collective-permute-done.5, pred[]{:T(512)S(6)} %eq.24), kind=kOutput, calls=%fused_computation.41 | convolution fusion | flops 2166358016 | bytes 13107205 | tf_op jit(solution)/shard_map/dot_general | solution.py:19
  87.5 0.2 reduce_max.55
  87.7 2.7 %multiply_reduce_fusion = (f32[512]{0:T(512)S(1)}, f32[512]{0:T(512)S(1)}, f32[512]{0:T(512)S(1)}) fusion(f32[512,1024]{1,0:T(8,128)S(1)} %fusion.30, f32[512,1024]{1,0:T(8,128)} %get-tuple-element.36, f32[512]{0:T(512)S(1)} %reduce_max.55, f32[512]{0:T(512)S(1)} %get-tuple-element.35), kind=kLoop, calls=%fused_computation.35 | loop fusion | flops 3668480 | bytes 4204544 | tf_op jit(solution)/shard_map/reduce_sum | solution.py:142
  90.5 9.9 %all_to_all.20 = f32[4,5,512]{2,1,0:T(8,128)S(1)} all-to-all(f32[4,5,512]{2,1,0:T(8,128)S(1)} %broadcast_in_dim.50), channel_id=1, replica_groups=mesh['x'=4,'core'=2,'z'=8,'y'=4] {'y'}, dimensions={0} | all-to-all | bytes 81920 | tf_op jit(solution)/shard_map/all_to_all | solution.py:23
  100.5 0.7 broadcast_in_dim.51
  101.1 8.5 %all-to-all-start.1 = ((f32[8,5,512]{2,1,0:T(8,128)}), f32[8,5,512]{2,1,0:T(8,128)S(1)}, u32[]{:S(2)}, u32[]{:S(2)}) async-start(f32[8,5,512]{2,1,0:T(8,128)} %broadcast_in_dim.51), calls=%async_computation.1 | async-start | bytes 262144 | tf_op jit(solution)/shard_map/all_to_all | solution.py:23
  109.6 3.9 %copy.54 = bf16[512,2048]{0,1:T(8,128)(2,1)} copy(bf16[512,2048]{1,0:T(8,128)(2,1)} %param.5) | data formatting | bytes 4194304 | tf_op args[0]
  113.6 5.1 %all-to-all-done.1 = f32[8,5,512]{2,1,0:T(8,128)S(1)} async-done(((f32[8,5,512]{2,1,0:T(8,128)}), f32[8,5,512]{2,1,0:T(8,128)S(1)}, u32[]{:S(2)}, u32[]{:S(2)}) %all-to-all-start.1) | async-done | bytes 81952 | tf_op jit(solution)/shard_map/all_to_all | solution.py:23
  118.7 0.1 slice_reduce_fusion.3
  118.8 0.6 add_multiply_fusion
  119.4 2.4 %multiply_convert_fusion = bf16[512,1024]{1,0:T(8,128)(2,1)S(1)} fusion(f32[512,1024]{1,0:T(8,128)S(1)} %fusion.30, f32[512,1024]{1,0:T(8,128)} %get-tuple-element.36, f32[512]{0:T(512)S(1)} %get-tuple-element.34, f32[512]{0:T(512)S(1)} %get-tuple-element.15, f32[512]{0:T(512)S(1)} %copy-done.3), kind=kLoop, calls=%fused_computation.34 | loop fusion | flops 2621440 | bytes 5249024 | tf_op jit(solution)/shard_map/convert_element_type | solution.py:152
  121.8 0.4 copy-done.5
  122.3 2.4 %convolution_convert_fusion = bf16[512,2048]{1,0:T(8,128)(2,1)S(1)} fusion(bf16[512,1024]{1,0:T(8,128)(2,1)S(1)} %multiply_convert_fusion, bf16[2048,1024]{1,0:T(8,128)(2,1)S(1)} %copy-done.5), kind=kOutput, calls=%fused_computation.33 | convolution fusion | flops 2148532224 | bytes 7340032 | tf_op jit(solution)/shard_map/dot_general | solution.py:19
  124.6 1.0 dynamic-slice_bitcast_fusion.5
  125.6 0.6 collective-permute-start.7
  126.2 2.1 collective-permute-start.8
  128.2 1.0 collective-permute-start.9
  129.2 1.2 constant_dynamic-slice_fusion
  130.4 2.6 %convolution_convert_fusion.1 = bf16[1024,1024]{1,0:T(8,128)(2,1)} fusion(bf16[512,1024]{0,1:T(8,128)(2,1)S(1)} %bitcast.151, bf16[512,1024]{1,0:T(8,128)(2,1)S(1)} %multiply_convert_fusion), kind=kOutput, calls=%fused_computation.39 | convolution fusion | flops 1074790400 | bytes 4194304 | tf_op jit(solution)/shard_map/dot_general | solution.py:19
  133.0 0.0 collective-permute-start.13
  133.0 16.8 %collective-permute-done.7 = bf16[128,2048]{1,0:T(8,128)(2,1)} collective-permute-done((bf16[128,2048]{1,0:T(8,128)(2,1)}, bf16[128,2048]{1,0:T(8,128)(2,1)}, u32[]{:S(2)}, u32[]{:S(2)}) %collective-permute-start.7) | collective-permute-done | bytes 524320 | tf_op jit(solution)/shard_map/ppermute | solution.py:15
  149.8 0.0 collective-permute-done.8
  149.9 0.4 collective-permute-done.9
  150.3 1.7 fusion.42
  152.0 19.2 %all_to_all.21 = bf16[8,16,2048]{2,1,0:T(8,128)(2,1)S(1)} all-to-all(bf16[8,16,2048]{2,1,0:T(8,128)(2,1)S(1)} %bitcast.149), channel_id=1, replica_groups=mesh['x'=4,'core'=2,'z'=8,'y'=4] {'z'}, dimensions={0} | all-to-all | bytes 1048576 | tf_op jit(solution)/shard_map/all_to_all | solution.py:23
  171.2 0.1 fusion.43
  171.3 0.8 broadcast_in_dim.53
  172.1 3.5 %all-to-all-start.3 = ((bf16[8,16,2048]{2,1,0:T(8,128)(2,1)}), bf16[8,16,2048]{2,1,0:T(8,128)(2,1)S(1)}, u32[]{:S(2)}, u32[]{:S(2)}) async-start(bf16[8,16,2048]{2,1,0:T(8,128)(2,1)} %broadcast_in_dim.53), calls=%async_computation.3 | async-start | bytes 1048576 | tf_op jit(solution)/shard_map/all_to_all | solution.py:23
  175.7 3.5 %add_convert_fusion = bf16[1024,1024]{1,0:T(8,128)(2,1)S(1)} fusion(bf16[1024,1024]{1,0:T(8,128)(2,1)} %collective-permute-done.13, bf16[512,1024]{0,1:T(8,128)(2,1)} %bitcast.150, bf16[512,1024]{1,0:T(8,128)(2,1)} %copy-done.2), kind=kOutput, calls=%fused_computation.28 | convolution fusion | flops 1076887552 | bytes 6291456 | tf_op jit(solution)/shard_map/dot_general | solution.py:19
  179.2 1.2 dynamic-slice_bitcast_fusion.2
  180.3 1.4 collective-permute-start.14
  181.7 2.6 %collective-permute-start.15 = (bf16[256,1024]{1,0:T(8,128)(2,1)}, bf16[256,1024]{1,0:T(8,128)(2,1)}, u32[]{:S(2)}, u32[]{:S(2)}) collective-permute-start(bf16[256,1024]{1,0:T(8,128)(2,1)} %get-tuple-element.18), channel_id=1, source_target_pairs={{0,128},{64,192},{128,0},{192,64},{1,129},{65,193},{129,1},{193,65... | collective-permute-start | bytes 1572872 | tf_op jit(solution)/shard_map/ppermute | solution.py:15
  184.3 1.3 collective-permute-start.16
  185.5 4.8 %all-to-all-done.3 = bf16[8,16,2048]{2,1,0:T(8,128)(2,1)S(1)} async-done(((bf16[8,16,2048]{2,1,0:T(8,128)(2,1)}), bf16[8,16,2048]{2,1,0:T(8,128)(2,1)S(1)}, u32[]{:S(2)}, u32[]{:S(2)}) %all-to-all-start.3) | async-done | bytes 524320 | tf_op jit(solution)/shard_map/all_to_all | solution.py:23
  190.3 3.5 %collective-permute-start.10 = (bf16[128,2048]{1,0:T(8,128)(2,1)S(1)}, bf16[128,2048]{1,0:T(8,128)(2,1)}, u32[]{:S(2)}, u32[]{:S(2)}) collective-permute-start(bf16[128,2048]{1,0:T(8,128)(2,1)S(1)} %bitcast.145), channel_id=1, source_target_pairs={{0,1},{1,2},{2,3},{3,0},{4,5},{5,6},{6,7},{7,4},{8,9},{9,10},{10,1... | collective-permute-start | bytes 1572872 | tf_op jit(solution)/shard_map/ppermute | solution.py:15
  193.8 3.3 %collective-permute-start.11 = (bf16[128,2048]{1,0:T(8,128)(2,1)S(1)}, bf16[128,2048]{1,0:T(8,128)(2,1)S(1)}, u32[]{:S(2)}, u32[]{:S(2)}) collective-permute-start(bf16[128,2048]{1,0:T(8,128)(2,1)S(1)} %bitcast.146), channel_id=1, source_target_pairs={{0,2},{1,3},{2,0},{3,1},{4,6},{5,7},{6,4},{7,5},{8,10},{9,11},{10,... | collective-permute-start | bytes 1572872 | tf_op jit(solution)/shard_map/ppermute | solution.py:15
  197.2 0.2 broadcast_in_dim.48
  197.4 0.1 bitcast_dynamic-update-slice_fusion.3
  197.5 0.0 collective-permute-done.14
  197.5 1.7 collective-permute-start.12
  199.2 5.8 %collective-permute-done.16 = bf16[256,1024]{1,0:T(8,128)(2,1)} collective-permute-done((bf16[256,1024]{1,0:T(8,128)(2,1)S(1)}, bf16[256,1024]{1,0:T(8,128)(2,1)}, u32[]{:S(2)}, u32[]{:S(2)}) %collective-permute-start.16) | collective-permute-done | bytes 524320 | tf_op jit(solution)/shard_map/ppermute | solution.py:15
  205.0 2.5 %fusion.39 = bf16[256,1024]{1,0:T(8,128)(2,1)} fusion(bf16[256,1024]{1,0:T(8,128)(2,1)} %collective-permute-done.16, bf16[256,1024]{1,0:T(8,128)(2,1)} %collective-permute-done.15, bf16[256,1024]{1,0:T(8,128)(2,1)} %collective-permute-done.14, bf16[4,256,1024]{2,1,0:T(8,128)(2,1)S(1)} %bitcast.142, s32[]{:T(128)S(6)} %select_n.171), kind=kLoop, calls=%fused_computation.51 | loop fusion | flops 2097152 | bytes 2621444 | tf_op jit(solution)/shard_map/convert_element_type | solution.py:100
  207.5 0.2 collective-permute-done.10
  207.7 1.1 bitcast_dynamic-update-slice_fusion.2
  208.8 9.3 %collective-permute-done.11 = bf16[128,2048]{1,0:T(8,128)(2,1)S(1)} collective-permute-done((bf16[128,2048]{1,0:T(8,128)(2,1)S(1)}, bf16[128,2048]{1,0:T(8,128)(2,1)S(1)}, u32[]{:S(2)}, u32[]{:S(2)}) %collective-permute-start.11) | collective-permute-done | bytes 524320 | tf_op jit(solution)/shard_map/ppermute | solution.py:15
  218.1 0.0 collective-permute-done.12
  218.2 0.0 copy-start.1
  218.2 1.3 copy-done.1
  (25 shorter events, 0.3 us)
Async XLA Ops:
  0.6 48.8 %collective-permute-start.2 = (bf16[8192,128]{1,0:T(8,128)(2,1)}, bf16[8192,128]{1,0:T(8,128)(2,1)}, u32[]{:S(2)}, u32[]{:S(2)}) collective-permute-start(bf16[8192,128]{1,0:T(8,128)(2,1)} %param.8), channel_id=1, source_target_pairs={{0,192},{32,96},{64,0},{96,160},{128,64},{160,224},{192,128},{224,... | collective-permute-start | bytes 6291464 | tf_op jit(solution)/shard_map/ppermute | solution.py:56
  2.9 46.5 %collective-permute-start.1 = (bf16[8192,128]{1,0:T(8,128)(2,1)}, bf16[8192,128]{1,0:T(8,128)(2,1)}, u32[]{:S(2)}, u32[]{:S(2)}) collective-permute-start(bf16[8192,128]{1,0:T(8,128)(2,1)} %param.8), channel_id=1, source_target_pairs={{0,64},{32,224},{64,128},{96,32},{128,192},{160,96},{192,0},{224,1... | collective-permute-start | bytes 6291464 | tf_op jit(solution)/shard_map/ppermute | solution.py:56
  3.0 54.5 %collective-permute-start = (bf16[8192,128]{1,0:T(8,128)(2,1)}, bf16[8192,128]{1,0:T(8,128)(2,1)}, u32[]{:S(2)}, u32[]{:S(2)}) collective-permute-start(bf16[8192,128]{1,0:T(8,128)(2,1)} %param.8), channel_id=1, source_target_pairs={{0,32},{32,0},{1,33},{33,1},{2,34},{34,2},{3,35},{35,3},{4,36},{36... | collective-permute-start | bytes 6291464 | tf_op jit(solution)/shard_map/ppermute | solution.py:15
  49.5 26.3 %collective-permute-start.3 = (bf16[8192,128]{1,0:T(8,128)(2,1)}, bf16[8192,128]{1,0:T(8,128)(2,1)S(1)}, u32[]{:S(2)}, u32[]{:S(2)}) collective-permute-start(bf16[8192,128]{1,0:T(8,128)(2,1)} %collective-permute-done.2), channel_id=1, source_target_pairs={{0,32},{32,0},{1,33},{33,1},{2,34},{34,2},{3,35},{35,3},{4,36},{36... | collective-permute-start | bytes 6291464 | tf_op jit(solution)/shard_map/ppermute | solution.py:15
  49.5 26.2 %collective-permute-start.5 = (bf16[8192,128]{1,0:T(8,128)(2,1)}, bf16[8192,128]{1,0:T(8,128)(2,1)S(1)}, u32[]{:S(2)}, u32[]{:S(2)}) collective-permute-start(bf16[8192,128]{1,0:T(8,128)(2,1)} %collective-permute-done.1), channel_id=1, source_target_pairs={{0,64},{32,224},{64,128},{96,32},{128,192},{160,96},{192,0},{224,1... | collective-permute-start | bytes 6291464 | tf_op jit(solution)/shard_map/ppermute | solution.py:56
  50.8 6.9 %copy-start.4 = (bf16[512,8192]{1,0:T(8,128)(2,1)S(1)}, bf16[512,8192]{1,0:T(8,128)(2,1)}, u32[]{:S(2)}) copy-start(bf16[512,8192]{1,0:T(8,128)(2,1)} %param.6) | copy-start | bytes 25165828
  57.4 1.6 copy-start.6
  57.4 23.0 %collective-permute-start.4 = (bf16[8192,128]{1,0:T(8,128)(2,1)}, bf16[8192,128]{1,0:T(8,128)(2,1)S(1)}, u32[]{:S(2)}, u32[]{:S(2)}) collective-permute-start(bf16[8192,128]{1,0:T(8,128)(2,1)} %collective-permute-done.1), channel_id=1, source_target_pairs={{0,32},{32,0},{1,33},{33,1},{2,34},{34,2},{3,35},{35,3},{4,36},{36... | collective-permute-start | bytes 6291464 | tf_op jit(solution)/shard_map/ppermute | solution.py:15
  75.7 9.4 %collective-permute-start.6 = (bf16[8192,128]{1,0:T(8,128)(2,1)S(1)}, bf16[8192,128]{1,0:T(8,128)(2,1)S(1)}, u32[]{:S(2)}, u32[]{:S(2)}) collective-permute-start(bf16[8192,128]{1,0:T(8,128)(2,1)S(1)} %collective-permute-done.5), channel_id=1, source_target_pairs={{0,32},{32,0},{1,33},{33,1},{2,34},{34,2},{3,35},{35,3},{4,36},{36... | collective-permute-start | bytes 6291464 | tf_op jit(solution)/shard_map/ppermute | solution.py:15
  101.1 17.5 %all-to-all-start.1 = ((f32[8,5,512]{2,1,0:T(8,128)}), f32[8,5,512]{2,1,0:T(8,128)S(1)}, u32[]{:S(2)}, u32[]{:S(2)}) async-start(f32[8,5,512]{2,1,0:T(8,128)} %broadcast_in_dim.51), calls=%async_computation.1 | async-start | bytes 262144 | tf_op jit(solution)/shard_map/all_to_all | solution.py:23
  109.6 9.2 %copy-start.3 = (f32[512]{0:T(512)S(1)}, f32[512]{0:T(512)}, u32[]{:S(2)}) copy-start(f32[512]{0:T(512)} %param.9) | copy-start | bytes 6148
  119.4 2.8 %copy-start.5 = (bf16[2048,1024]{1,0:T(8,128)(2,1)S(1)}, bf16[2048,1024]{1,0:T(8,128)(2,1)}, u32[]{:S(2)}) copy-start(bf16[2048,1024]{1,0:T(8,128)(2,1)} %param.7) | copy-start | bytes 12582916
  122.3 8.2 %copy-start.2 = (bf16[512,1024]{1,0:T(8,128)(2,1)}, bf16[512,1024]{1,0:T(8,128)(2,1)S(1)}, u32[]{:S(2)}) copy-start(bf16[512,1024]{1,0:T(8,128)(2,1)S(1)} %multiply_convert_fusion) | copy-start | bytes 3145732
  124.6 4.6 %copy-start = (bf16[512,2048]{0,1:T(8,128)(2,1)S(1)}, bf16[512,2048]{0,1:T(8,128)(2,1)}, u32[]{:S(2)}) copy-start(bf16[512,2048]{0,1:T(8,128)(2,1)} %copy.54) | copy-start | bytes 6291460
  125.6 24.2 %collective-permute-start.7 = (bf16[128,2048]{1,0:T(8,128)(2,1)}, bf16[128,2048]{1,0:T(8,128)(2,1)}, u32[]{:S(2)}, u32[]{:S(2)}) collective-permute-start(bf16[128,2048]{1,0:T(8,128)(2,1)} %get-tuple-element.21), channel_id=1, source_target_pairs={{0,1},{1,2},{2,3},{3,0},{4,5},{5,6},{6,7},{7,4},{8,9},{9,10},{10,1... | collective-permute-start | bytes 1572872 | tf_op jit(solution)/shard_map/ppermute | solution.py:15
  126.2 23.7 %collective-permute-start.8 = (bf16[128,2048]{1,0:T(8,128)(2,1)S(1)}, bf16[128,2048]{1,0:T(8,128)(2,1)}, u32[]{:S(2)}, u32[]{:S(2)}) collective-permute-start(bf16[128,2048]{1,0:T(8,128)(2,1)S(1)} %get-tuple-element.23), channel_id=1, source_target_pairs={{0,2},{1,3},{2,0},{3,1},{4,6},{5,7},{6,4},{7,5},{8,10},{9,11},{10,... | collective-permute-start | bytes 1572872 | tf_op jit(solution)/shard_map/ppermute | solution.py:15
  128.2 22.0 %collective-permute-start.9 = (bf16[128,2048]{1,0:T(8,128)(2,1)S(1)}, bf16[128,2048]{1,0:T(8,128)(2,1)}, u32[]{:S(2)}, u32[]{:S(2)}) collective-permute-start(bf16[128,2048]{1,0:T(8,128)(2,1)S(1)} %get-tuple-element.22), channel_id=1, source_target_pairs={{0,3},{1,0},{2,1},{3,2},{4,7},{5,4},{6,5},{7,6},{8,11},{9,8},{10,9... | collective-permute-start | bytes 1572872 | tf_op jit(solution)/shard_map/ppermute | solution.py:15
  133.0 42.6 %collective-permute-start.13 = (bf16[1024,1024]{1,0:T(8,128)(2,1)}, bf16[1024,1024]{1,0:T(8,128)(2,1)}, u32[]{:S(2)}, u32[]{:S(2)}) collective-permute-start(bf16[1024,1024]{1,0:T(8,128)(2,1)} %convolution_convert_fusion.1), channel_id=1, source_target_pairs={{0,32},{32,0},{1,33},{33,1},{2,34},{34,2},{3,35},{35,3},{4,36},{36... | collective-permute-start | bytes 6291464 | tf_op jit(solution)/shard_map/ppermute | solution.py:15
  172.1 18.2 %all-to-all-start.3 = ((bf16[8,16,2048]{2,1,0:T(8,128)(2,1)}), bf16[8,16,2048]{2,1,0:T(8,128)(2,1)S(1)}, u32[]{:S(2)}, u32[]{:S(2)}) async-start(bf16[8,16,2048]{2,1,0:T(8,128)(2,1)} %broadcast_in_dim.53), calls=%async_computation.3 | async-start | bytes 1048576 | tf_op jit(solution)/shard_map/all_to_all | solution.py:23
  180.3 17.2 %collective-permute-start.14 = (bf16[256,1024]{1,0:T(8,128)(2,1)}, bf16[256,1024]{1,0:T(8,128)(2,1)}, u32[]{:S(2)}, u32[]{:S(2)}) collective-permute-start(bf16[256,1024]{1,0:T(8,128)(2,1)} %get-tuple-element.16), channel_id=1, source_target_pairs={{0,64},{64,128},{128,192},{192,0},{1,65},{65,129},{129,193},{193,1... | collective-permute-start | bytes 1572872 | tf_op jit(solution)/shard_map/ppermute | solution.py:15
  181.7 17.6 %collective-permute-start.15 = (bf16[256,1024]{1,0:T(8,128)(2,1)}, bf16[256,1024]{1,0:T(8,128)(2,1)}, u32[]{:S(2)}, u32[]{:S(2)}) collective-permute-start(bf16[256,1024]{1,0:T(8,128)(2,1)} %get-tuple-element.18), channel_id=1, source_target_pairs={{0,128},{64,192},{128,0},{192,64},{1,129},{65,193},{129,1},{193,65... | collective-permute-start | bytes 1572872 | tf_op jit(solution)/shard_map/ppermute | solution.py:15
  184.3 20.7 %collective-permute-start.16 = (bf16[256,1024]{1,0:T(8,128)(2,1)S(1)}, bf16[256,1024]{1,0:T(8,128)(2,1)}, u32[]{:S(2)}, u32[]{:S(2)}) collective-permute-start(bf16[256,1024]{1,0:T(8,128)(2,1)S(1)} %get-tuple-element.17), channel_id=1, source_target_pairs={{0,192},{64,0},{128,64},{192,128},{1,193},{65,1},{129,65},{193,129... | collective-permute-start | bytes 1572872 | tf_op jit(solution)/shard_map/ppermute | solution.py:15
  190.3 17.4 %collective-permute-start.10 = (bf16[128,2048]{1,0:T(8,128)(2,1)S(1)}, bf16[128,2048]{1,0:T(8,128)(2,1)}, u32[]{:S(2)}, u32[]{:S(2)}) collective-permute-start(bf16[128,2048]{1,0:T(8,128)(2,1)S(1)} %bitcast.145), channel_id=1, source_target_pairs={{0,1},{1,2},{2,3},{3,0},{4,5},{5,6},{6,7},{7,4},{8,9},{9,10},{10,1... | collective-permute-start | bytes 1572872 | tf_op jit(solution)/shard_map/ppermute | solution.py:15
  193.8 24.2 %collective-permute-start.11 = (bf16[128,2048]{1,0:T(8,128)(2,1)S(1)}, bf16[128,2048]{1,0:T(8,128)(2,1)S(1)}, u32[]{:S(2)}, u32[]{:S(2)}) collective-permute-start(bf16[128,2048]{1,0:T(8,128)(2,1)S(1)} %bitcast.146), channel_id=1, source_target_pairs={{0,2},{1,3},{2,0},{3,1},{4,6},{5,7},{6,4},{7,5},{8,10},{9,11},{10,... | collective-permute-start | bytes 1572872 | tf_op jit(solution)/shard_map/ppermute | solution.py:15
  197.5 20.6 %collective-permute-start.12 = (bf16[128,2048]{1,0:T(8,128)(2,1)S(1)}, bf16[128,2048]{1,0:T(8,128)(2,1)S(1)}, u32[]{:S(2)}, u32[]{:S(2)}) collective-permute-start(bf16[128,2048]{1,0:T(8,128)(2,1)S(1)} %bitcast.148), channel_id=1, source_target_pairs={{0,3},{1,0},{2,1},{3,2},{4,7},{5,4},{6,5},{7,6},{8,11},{9,8},{10,9... | collective-permute-start | bytes 1572872 | tf_op jit(solution)/shard_map/ppermute | solution.py:15
  218.2 1.3 copy-start.1
where the time goes:
time: 221 us; the launch traced here: 220 us
  waiting for transfers between devices  101 us (46%)
  starting transfers between devices  33.1 us (15%)
  matrix products  31.5 us (14%)
  blocking collectives  29.1 us (13%)
  local copies, waits for them, and re-layouts  13.6 us (6%)
  other arithmetic  10.4 us (5%)
    ppermute x3, waiting for transfers between devices, turned(): return lax.ppermute(piece, ROWS, pairs)  58.5 us
    ppermute x14, waiting for transfers between devices, shifted(): return lax.ppermute(x, axis, [(i, (i + by) % n) for i in range(n)])  32.5 us
    dot_general x8, matrix products, dot(): lax.dot_general(a, b, (contract, ((), ())), preferred_element_type=jnp.fl...  31.5 us
    all_to_all x2, blocking collectives, exchanged(): return lax.all_to_all(pieces, axis, 0, 0, tiled=True)  29.1 us
    ppermute x14, starting transfers between devices, shifted(): return lax.ppermute(x, axis, [(i, (i + by) % n) for i in range(n)])  17.4 us
    all_to_all x2, starting transfers between devices, exchanged(): return lax.all_to_all(pieces, axis, 0, 0, tiled=True)  12 us
    all_to_all x2, waiting for transfers between devices, exchanged(): return lax.all_to_all(pieces, axis, 0, 0, tiled=True)  9.93 us
    unnamed x15, local copies, waits for them, and re-layouts  7 us
  transfers between devices with their start and end apart: 19, of which 9 were waited for; matrix products, arithmetic and copies ran while one was open for 18% of the time, Pallas kernels for 0%

commit v1 on v0

--- a/solution.py
+++ b/solution.py
@@ -43,19 +43,23 @@
     )
 
 
+def turned(piece, axis, way):
+    ring = lax.axis_size(axis)
+    axes = (axis, "core") if axis == "x" else ("core", axis)
+
+    def at(i, c):
+        return 2 * (i % ring) + c if axis == "x" else ring * c + i % ring
+
+    pairs = [(at(i, c), at(i + (way, -way)[c], c)) for i in range(ring) for c in range(2)]
+    return lax.ppermute(piece, axes, pairs)
+
+
 def teacher_product(hidden, own):
     place, core = lax.axis_index("x"), lax.axis_index("core")
     ring = lax.axis_size("x")
+    half = own.shape[0] // 2
 
-    def turned(piece, way):
-        pairs = [
-            (2 * i + c, 2 * ((i + (way if c == 0 else -way)) % ring) + c)
-            for i in range(ring)
-            for c in range(2)
-        ]
-        return lax.ppermute(piece, ROWS, pairs)
-
-    def product(mine, others):
+    def product(hidden, mine, others):
         pair = jnp.where(
             core == 0,
             jnp.concatenate([mine, others], axis=1),
@@ -63,12 +67,14 @@
         )
         return dot(hidden, pair, ((1,), (0,)))
 
-    behind, ahead = turned(own, 1), turned(own, -1)
-    far = turned(behind, 1)
-    own_part = product(own, shifted(own, "core", 1))
-    behind_part = product(behind, shifted(ahead, "core", 1))
-    ahead_part = product(ahead, shifted(behind, "core", 1))
-    far_part = product(far, shifted(far, "core", 1))
+    behind, ahead = turned(own, "x", 1), turned(own, "x", -1)
+    far_top = turned(behind[:half], "x", 1)
+    far_low = turned(behind[half:], "x", 1)
+    own_part = product(hidden, own, shifted(own, "core", 1))
+    behind_part = product(hidden, behind, shifted(ahead, "core", 1))
+    ahead_part = product(hidden, ahead, shifted(behind, "core", 1))
+    far_part = product(hidden[:, :half], far_top, shifted(far_top, "core", 1))
+    far_part = far_part + product(hidden[:, half:], far_low, shifted(far_low, "core", 1))
     width = 2 * own.shape[1]
     back = jnp.where(core == 0, ring - 1, 1)
     logits = jnp.zeros((hidden.shape[0], ring * width), jnp.float32)
@@ -88,11 +94,13 @@
 
 
 def gathered(block, axis):
-    n, place = lax.axis_size(axis), lax.axis_index(axis)
+    n, place, core = lax.axis_size(axis), lax.axis_index(axis), lax.axis_index("core")
+    back = jnp.where(core == 0, n - 1, 1)
+    behind, ahead = turned(block, axis, 1), turned(block, axis, -1)
+    far = turned(behind, axis, 1)
     whole = jnp.zeros((n, *block.shape), block.dtype)
-    for by in range(n):
-        piece = shifted(block, axis, by) if by else block
-        whole = lax.dynamic_update_index_in_dim(whole, piece, (place - by) % n, 0)
+    for step, piece in ((0, block), (back, behind), (n - back, ahead), (2, far)):
+        whole = lax.dynamic_update_index_in_dim(whole, piece, (place + step) % n, 0)
     return whole
 
 

time: 221 us -> 225 us (1.018)
  waiting for transfers between devices: 101 us -> 107 us
  starting transfers between devices: 33.1 us -> 29.6 us
    ppermute x14 -> x12, starting transfers between devices: 17.4 us -> 9.02 us  [shifted(): return lax.ppermute(x, axis, [(i, (i + by) % n) for i in range(n)])]
    ppermute x3 -> x7, waiting for transfers between devices: 58.5 us -> 66.9 us  [turned(): return lax.ppermute(piece, axes, pairs)]
    ppermute x3 -> x7, starting transfers between devices: 3.67 us -> 8.57 us  [turned(): return lax.ppermute(piece, axes, pairs)]
    ppermute x14 -> x12, waiting for transfers between devices: 32.5 us -> 28.8 us  [shifted(): return lax.ppermute(x, axis, [(i, (i + by) % n) for i in range(n)])]
    dot_general x8 -> x9, matrix products: 31.5 us -> 31.7 us  [dot(): lax.dot_general(a, b, (contract, ((), ())), preferred_element_type=jnp.fl...]
  transfers between devices with their start and end apart: 19 -> 21, of which waited for: 9 -> 11; matrix products, arithmetic and copies ran while one was open for 18% -> 19% of each run, Pallas kernels for 0% -> 0%
where the time goes in v1:
time: 225 us; the launch traced here: 224 us
  waiting for transfers between devices  107 us (48%)
  matrix products  31.7 us (14%)
  blocking collectives  30.3 us (13%)
  starting transfers between devices  29.6 us (13%)
  local copies, waits for them, and re-layouts  14 us (6%)
  other arithmetic  10.4 us (5%)
    ppermute x7, waiting for transfers between devices, turned(): return lax.ppermute(piece, axes, pairs)  66.9 us
    dot_general x9, matrix products, dot(): lax.dot_general(a, b, (contract, ((), ())), preferred_element_type=jnp.fl...  31.7 us
    all_to_all x2, blocking collectives, exchanged(): return lax.all_to_all(pieces, axis, 0, 0, tiled=True)  30.3 us
    ppermute x12, waiting for transfers between devices, shifted(): return lax.ppermute(x, axis, [(i, (i + by) % n) for i in range(n)])  28.8 us
    all_to_all x2, starting transfers between devices, exchanged(): return lax.all_to_all(pieces, axis, 0, 0, tiled=True)  12 us
    all_to_all x2, waiting for transfers between devices, exchanged(): return lax.all_to_all(pieces, axis, 0, 0, tiled=True)  11.5 us
    ppermute x12, starting transfers between devices, shifted(): return lax.ppermute(x, axis, [(i, (i + by) % n) for i in range(n)])  9.02 us
    ppermute x7, starting transfers between devices, turned(): return lax.ppermute(piece, axes, pairs)  8.57 us
  transfers between devices with their start and end apart: 21, of which 11 were waited for; matrix products, arithmetic and copies ran while one was open for 19% of the time, Pallas kernels for 0%

profile of v1, /device:TPU:2, one launch (start us, length us, event | category | flops | bytes accessed | tf_op | source)
XLA Modules:
  0.0 224.0 jit_solution(1839207544438751804)
XLA Ops:
  0.6 2.3 %collective-permute-start.2 = (bf16[8192,128]{1,0:T(8,128)(2,1)}, bf16[8192,128]{1,0:T(8,128)(2,1)}, u32[]{:S(2)}, u32[]{:S(2)}) collective-permute-start(bf16[8192,128]{1,0:T(8,128)(2,1)} %param.8), channel_id=1, source_target_pairs={{0,192},{32,96},{64,0},{96,160},{128,64},{160,224},{192,128},{224,... | collective-permute-start | bytes 6291464 | tf_op jit(solution)/shard_map/ppermute | solution.py:54
  3.0 6.6 %fusion.84 = (f32[512]{0:T(512)S(1)}, f32[512,1024]{1,0:T(8,128)}) fusion(bf16[512,2048]{1,0:T(8,128)(2,1)} %param.5, bf16[2048,1024]{1,0:T(8,128)(2,1)} %param.7), kind=kOutput, calls=%fused_computation.120 | convolution fusion | flops 2148007424 | bytes 8390656 | tf_op jit(solution)/shard_map/dot_general | solution.py:19
  9.6 39.9 %collective-permute-done.2 = bf16[8192,128]{1,0:T(8,128)(2,1)} collective-permute-done((bf16[8192,128]{1,0:T(8,128)(2,1)}, bf16[8192,128]{1,0:T(8,128)(2,1)}, u32[]{:S(2)}, u32[]{:S(2)}) %collective-permute-start.2) | collective-permute-done | bytes 2097184 | tf_op jit(solution)/shard_map/ppermute | solution.py:54
  49.5 0.0 collective-permute-start.3
  49.5 0.0 collective-permute-done.1
  49.5 1.7 fusion.83
  51.1 0.0 copy-start.6
  51.2 1.4 collective-permute-start.7
  52.6 1.6 collective-permute-start.5
  54.2 0.6 collective-permute-start.4
  54.7 0.2 broadcast_in_dim.49
  55.0 4.7 %fusion.43 = f32[512,1024]{1,0:T(8,128)S(1)} fusion(f32[512,1024]{1,0:T(8,128)S(1)} %broadcast_in_dim.49, s32[]{:T(128)S(6)} %select_n.149, bf16[512,8192]{1,0:T(8,128)(2,1)S(1)} %copy-done.4, bf16[8192,128]{1,0:T(8,128)(2,1)} %collective-permute-done, bf16[8192,128]{1,0:T(8,128)(2,1)S(1)} %copy-done.6, pred[]{:T(512)S(6)} %eq.26), kind=kOutput, calls=%fused_computation.55 | convolution fusion | flops 2166358016 | bytes 13107205 | tf_op jit(solution)/shard_map/dot_general | solution.py:19
  59.7 6.4 %collective-permute-done.7 = bf16[4096,128]{1,0:T(8,128)(2,1)S(1)} collective-permute-done((bf16[4096,128]{1,0:T(8,128)(2,1)S(1)}, bf16[4096,128]{1,0:T(8,128)(2,1)S(1)}, u32[]{:S(2)}, u32[]{:S(2)}) %collective-permute-start.7) | collective-permute-done | bytes 1048608 | tf_op jit(solution)/shard_map/ppermute | solution.py:54
  66.0 0.0 collective-permute-start.8
  66.0 11.2 %collective-permute-done.5 = bf16[4096,128]{1,0:T(8,128)(2,1)S(1)} collective-permute-done((bf16[4096,128]{1,0:T(8,128)(2,1)S(1)}, bf16[4096,128]{1,0:T(8,128)(2,1)S(1)}, u32[]{:S(2)}, u32[]{:S(2)}) %collective-permute-start.5) | collective-permute-done | bytes 1048608 | tf_op jit(solution)/shard_map/ppermute | solution.py:54
  77.3 0.0 collective-permute-start.6
  77.3 4.7 %fusion.41 = f32[512,1024]{1,0:T(8,128)S(1)} fusion(f32[512,1024]{1,0:T(8,128)S(1)} %fusion.43, s32[]{:T(128)S(6)} %select_n.153, bf16[512,8192]{1,0:T(8,128)(2,1)S(1)} %copy-done.4, bf16[8192,128]{1,0:T(8,128)(2,1)S(1)} %collective-permute-done.3, bf16[8192,128]{1,0:T(8,128)(2,1)} %collective-permute-done.1, pred[]{:T(512)S(6)} %eq.26), kind=kOutput, calls=%fused_computation.53 | convolution fusion | flops 2166358016 | bytes 13107205 | tf_op jit(solution)/shard_map/dot_general | solution.py:19
  82.0 4.7 %fusion.39 = f32[512,1024]{1,0:T(8,128)S(1)} fusion(f32[512,1024]{1,0:T(8,128)S(1)} %fusion.41, s32[]{:T(128)S(6)} %select_n.156, bf16[512,8192]{1,0:T(8,128)(2,1)S(1)} %copy-done.4, bf16[8192,128]{1,0:T(8,128)(2,1)S(1)} %collective-permute-done.4, bf16[8192,128]{1,0:T(8,128)(2,1)} %collective-permute-done.2, pred[]{:T(512)S(6)} %eq.26), kind=kOutput, calls=%fused_computation.51 | convolution fusion | flops 2166358016 | bytes 13107205 | tf_op jit(solution)/shard_map/dot_general | solution.py:19
  86.7 0.0 collective-permute-done.8
  86.7 1.3 fusion.18
  88.0 1.3 fusion.50
  89.3 0.2 reduce_max.55
  89.4 2.7 %multiply_reduce_fusion = (f32[512]{0:T(512)S(1)}, f32[512]{0:T(512)S(1)}, f32[512]{0:T(512)S(1)}) fusion(f32[512,1024]{1,0:T(8,128)S(1)} %fusion.50, f32[512,1024]{1,0:T(8,128)} %get-tuple-element.38, f32[512]{0:T(512)S(1)} %reduce_max.55, f32[512]{0:T(512)S(1)} %get-tuple-element.37), kind=kLoop, calls=%fused_computation.43 | loop fusion | flops 3668480 | bytes 4204544 | tf_op jit(solution)/shard_map/reduce_sum | solution.py:150
  92.2 9.9 %all_to_all.20 = f32[4,5,512]{2,1,0:T(8,128)S(1)} all-to-all(f32[4,5,512]{2,1,0:T(8,128)S(1)} %broadcast_in_dim.50), channel_id=1, replica_groups=mesh['x'=4,'core'=2,'z'=8,'y'=4] {'y'}, dimensions={0} | all-to-all | bytes 81920 | tf_op jit(solution)/shard_map/all_to_all | solution.py:23
  102.2 0.7 broadcast_in_dim.51
  102.9 8.5 %all-to-all-start.1 = ((f32[8,5,512]{2,1,0:T(8,128)}), f32[8,5,512]{2,1,0:T(8,128)S(1)}, u32[]{:S(2)}, u32[]{:S(2)}) async-start(f32[8,5,512]{2,1,0:T(8,128)} %broadcast_in_dim.51), calls=%async_computation.1 | async-start | bytes 262144 | tf_op jit(solution)/shard_map/all_to_all | solution.py:23
  111.3 3.9 %copy.59 = bf16[512,2048]{0,1:T(8,128)(2,1)} copy(bf16[512,2048]{1,0:T(8,128)(2,1)} %param.5) | data formatting | bytes 4194304 | tf_op args[0]
  115.3 5.1 %all-to-all-done.1 = f32[8,5,512]{2,1,0:T(8,128)S(1)} async-done(((f32[8,5,512]{2,1,0:T(8,128)}), f32[8,5,512]{2,1,0:T(8,128)S(1)}, u32[]{:S(2)}, u32[]{:S(2)}) %all-to-all-start.1) | async-done | bytes 81952 | tf_op jit(solution)/shard_map/all_to_all | solution.py:23
  120.4 0.1 slice_reduce_fusion.3
  120.6 0.6 add_multiply_fusion
  121.2 2.4 %multiply_convert_fusion = bf16[512,1024]{1,0:T(8,128)(2,1)S(1)} fusion(f32[512,1024]{1,0:T(8,128)S(1)} %fusion.50, f32[512,1024]{1,0:T(8,128)} %get-tuple-element.38, f32[512]{0:T(512)S(1)} %get-tuple-element.36, f32[512]{0:T(512)S(1)} %get-tuple-element.15, f32[512]{0:T(512)S(1)} %copy-done.3), kind=kLoop, calls=%fused_computation.42 | loop fusion | flops 2621440 | bytes 5249024 | tf_op jit(solution)/shard_map/convert_element_type | solution.py:160
  123.6 0.4 copy-done.5
  124.0 2.4 %convolution_convert_fusion = bf16[512,2048]{1,0:T(8,128)(2,1)S(1)} fusion(bf16[512,1024]{1,0:T(8,128)(2,1)S(1)} %multiply_convert_fusion, bf16[2048,1024]{1,0:T(8,128)(2,1)S(1)} %copy-done.5), kind=kOutput, calls=%fused_computation.29 | convolution fusion | flops 2148532224 | bytes 7340032 | tf_op jit(solution)/shard_map/dot_general | solution.py:19
  126.4 1.0 dynamic-slice_bitcast_fusion.5
  127.3 1.0 collective-permute-start.10
  128.3 2.2 %collective-permute-start.11 = (bf16[128,2048]{1,0:T(8,128)(2,1)S(1)}, bf16[128,2048]{1,0:T(8,128)(2,1)}, u32[]{:S(2)}, u32[]{:S(2)}) collective-permute-start(bf16[128,2048]{1,0:T(8,128)(2,1)S(1)} %get-tuple-element.22), channel_id=1, source_target_pairs={{0,3},{1,0},{2,1},{3,2},{4,7},{5,4},{6,5},{7,6},{8,11},{9,8},{10,9... | collective-permute-start | bytes 1572872 | tf_op jit(solution)/shard_map/ppermute | solution.py:15
  130.6 0.0 collective-permute-start.9
  130.6 1.2 constant_dynamic-slice_fusion
  131.8 2.6 %convolution_convert_fusion.1 = bf16[1024,1024]{1,0:T(8,128)(2,1)} fusion(bf16[512,1024]{0,1:T(8,128)(2,1)S(1)} %bitcast.149, bf16[512,1024]{1,0:T(8,128)(2,1)S(1)} %multiply_convert_fusion), kind=kOutput, calls=%fused_computation.49 | convolution fusion | flops 1074790400 | bytes 4194304 | tf_op jit(solution)/shard_map/dot_general | solution.py:19
  134.4 9.6 %collective-permute-done.10 = bf16[128,2048]{1,0:T(8,128)(2,1)} collective-permute-done((bf16[128,2048]{1,0:T(8,128)(2,1)}, bf16[128,2048]{1,0:T(8,128)(2,1)}, u32[]{:S(2)}, u32[]{:S(2)}) %collective-permute-start.10) | collective-permute-done | bytes 524320 | tf_op jit(solution)/shard_map/ppermute | solution.py:15
  144.0 6.4 %collective-permute-done.11 = bf16[128,2048]{1,0:T(8,128)(2,1)} collective-permute-done((bf16[128,2048]{1,0:T(8,128)(2,1)S(1)}, bf16[128,2048]{1,0:T(8,128)(2,1)}, u32[]{:S(2)}, u32[]{:S(2)}) %collective-permute-start.11) | collective-permute-done | bytes 524320 | tf_op jit(solution)/shard_map/ppermute | solution.py:15
  150.4 1.5 collective-permute-done.9
  151.9 1.7 fusion.58
  153.6 20.4 %all_to_all.21 = bf16[8,16,2048]{2,1,0:T(8,128)(2,1)S(1)} all-to-all(bf16[8,16,2048]{2,1,0:T(8,128)(2,1)S(1)} %bitcast.147), channel_id=1, replica_groups=mesh['x'=4,'core'=2,'z'=8,'y'=4] {'z'}, dimensions={0} | all-to-all | bytes 1048576 | tf_op jit(solution)/shard_map/all_to_all | solution.py:23
  174.0 0.1 fusion.59
  174.1 0.8 broadcast_in_dim.53
  174.9 3.5 %all-to-all-start.3 = ((bf16[8,16,2048]{2,1,0:T(8,128)(2,1)}), bf16[8,16,2048]{2,1,0:T(8,128)(2,1)S(1)}, u32[]{:S(2)}, u32[]{:S(2)}) async-start(bf16[8,16,2048]{2,1,0:T(8,128)(2,1)} %broadcast_in_dim.53), calls=%async_computation.3 | async-start | bytes 1048576 | tf_op jit(solution)/shard_map/all_to_all | solution.py:23
  178.4 3.5 %add_convert_fusion = bf16[1024,1024]{1,0:T(8,128)(2,1)S(1)} fusion(bf16[1024,1024]{1,0:T(8,128)(2,1)} %collective-permute-done.15, bf16[512,1024]{0,1:T(8,128)(2,1)} %bitcast.148, bf16[512,1024]{1,0:T(8,128)(2,1)} %copy-done.2), kind=kOutput, calls=%fused_computation.21 | convolution fusion | flops 1076887552 | bytes 6291456 | tf_op jit(solution)/shard_map/dot_general | solution.py:19
  181.9 1.2 dynamic-slice_bitcast_fusion.2
  183.1 1.3 collective-permute-start.16
  184.4 2.6 %collective-permute-start.17 = (bf16[256,1024]{1,0:T(8,128)(2,1)}, bf16[256,1024]{1,0:T(8,128)(2,1)}, u32[]{:S(2)}, u32[]{:S(2)}) collective-permute-start(bf16[256,1024]{1,0:T(8,128)(2,1)} %get-tuple-element.18), channel_id=1, source_target_pairs={{0,128},{64,192},{128,0},{192,64},{1,129},{65,193},{129,1},{193,65... | collective-permute-start | bytes 1572872 | tf_op jit(solution)/shard_map/ppermute | solution.py:15
  187.1 1.3 collective-permute-start.18
  188.3 6.4 %all-to-all-done.3 = bf16[8,16,2048]{2,1,0:T(8,128)(2,1)S(1)} async-done(((bf16[8,16,2048]{2,1,0:T(8,128)(2,1)}), bf16[8,16,2048]{2,1,0:T(8,128)(2,1)S(1)}, u32[]{:S(2)}, u32[]{:S(2)}) %all-to-all-start.3) | async-done | bytes 524320 | tf_op jit(solution)/shard_map/all_to_all | solution.py:23
  194.7 3.2 %collective-permute-start.13 = (bf16[128,2048]{1,0:T(8,128)(2,1)S(1)}, bf16[128,2048]{1,0:T(8,128)(2,1)S(1)}, u32[]{:S(2)}, u32[]{:S(2)}) collective-permute-start(bf16[128,2048]{1,0:T(8,128)(2,1)S(1)} %bitcast.145), channel_id=1, source_target_pairs={{0,3},{32,33},{1,0},{33,34},{2,1},{34,35},{3,2},{35,32},{4,7},{36,... | collective-permute-start | bytes 1572872 | tf_op jit(solution)/shard_map/ppermute | solution.py:54
  197.9 0.2 broadcast_in_dim.48
  198.2 0.1 bitcast_dynamic-update-slice_fusion.3
  198.2 2.8 %collective-permute-done.17 = bf16[256,1024]{1,0:T(8,128)(2,1)} collective-permute-done((bf16[256,1024]{1,0:T(8,128)(2,1)}, bf16[256,1024]{1,0:T(8,128)(2,1)}, u32[]{:S(2)}, u32[]{:S(2)}) %collective-permute-start.17) | collective-permute-done | bytes 524320 | tf_op jit(solution)/shard_map/ppermute | solution.py:15
  201.1 8.4 %collective-permute-done.18 = bf16[256,1024]{1,0:T(8,128)(2,1)} collective-permute-done((bf16[256,1024]{1,0:T(8,128)(2,1)S(1)}, bf16[256,1024]{1,0:T(8,128)(2,1)}, u32[]{:S(2)}, u32[]{:S(2)}) %collective-permute-start.18) | collective-permute-done | bytes 524320 | tf_op jit(solution)/shard_map/ppermute | solution.py:15
  209.5 2.5 %fusion.55 = bf16[256,1024]{1,0:T(8,128)(2,1)} fusion(bf16[256,1024]{1,0:T(8,128)(2,1)} %collective-permute-done.18, bf16[256,1024]{1,0:T(8,128)(2,1)} %collective-permute-done.17, bf16[256,1024]{1,0:T(8,128)(2,1)} %collective-permute-done.16, bf16[4,256,1024]{2,1,0:T(8,128)(2,1)S(1)} %bitcast.141, s32[]{:T(128)S(6)} %select_n.176), kind=kLoop, calls=%fused_computation.62 | loop fusion | flops 2097152 | bytes 2621444 | tf_op jit(solution)/shard_map/convert_element_type | solution.py:108
  212.0 1.1 bitcast_dynamic-update-slice_fusion.2
  213.1 0.1 bitcast_dynamic-update-slice_fusion.1
  213.2 9.4 %collective-permute-done.14 = bf16[128,2048]{1,0:T(8,128)(2,1)S(1)} collective-permute-done((bf16[128,2048]{1,0:T(8,128)(2,1)}, bf16[128,2048]{1,0:T(8,128)(2,1)S(1)}, u32[]{:S(2)}, u32[]{:S(2)}) %collective-permute-start.14) | collective-permute-done | bytes 524320 | tf_op jit(solution)/shard_map/ppermute | solution.py:54
  222.7 0.0 copy-start.1
  222.7 1.3 copy-done.1
  (31 shorter events, 0.3 us)
Async XLA Ops:
  0.6 48.8 %collective-permute-start.2 = (bf16[8192,128]{1,0:T(8,128)(2,1)}, bf16[8192,128]{1,0:T(8,128)(2,1)}, u32[]{:S(2)}, u32[]{:S(2)}) collective-permute-start(bf16[8192,128]{1,0:T(8,128)(2,1)} %param.8), channel_id=1, source_target_pairs={{0,192},{32,96},{64,0},{96,160},{128,64},{160,224},{192,128},{224,... | collective-permute-start | bytes 6291464 | tf_op jit(solution)/shard_map/ppermute | solution.py:54
  2.9 46.5 %collective-permute-start.1 = (bf16[8192,128]{1,0:T(8,128)(2,1)}, bf16[8192,128]{1,0:T(8,128)(2,1)}, u32[]{:S(2)}, u32[]{:S(2)}) collective-permute-start(bf16[8192,128]{1,0:T(8,128)(2,1)} %param.8), channel_id=1, source_target_pairs={{0,64},{32,224},{64,128},{96,32},{128,192},{160,96},{192,0},{224,1... | collective-permute-start | bytes 6291464 | tf_op jit(solution)/shard_map/ppermute | solution.py:54
  3.0 51.8 %collective-permute-start = (bf16[8192,128]{1,0:T(8,128)(2,1)}, bf16[8192,128]{1,0:T(8,128)(2,1)}, u32[]{:S(2)}, u32[]{:S(2)}) collective-permute-start(bf16[8192,128]{1,0:T(8,128)(2,1)} %param.8), channel_id=1, source_target_pairs={{0,32},{32,0},{1,33},{33,1},{2,34},{34,2},{3,35},{35,3},{4,36},{36... | collective-permute-start | bytes 6291464 | tf_op jit(solution)/shard_map/ppermute | solution.py:15
  3.0 52.0 %copy-start.4 = (bf16[512,8192]{1,0:T(8,128)(2,1)S(1)}, bf16[512,8192]{1,0:T(8,128)(2,1)}, u32[]{:S(2)}) copy-start(bf16[512,8192]{1,0:T(8,128)(2,1)} %param.6) | copy-start | bytes 25165828
  49.5 27.8 %collective-permute-start.3 = (bf16[8192,128]{1,0:T(8,128)(2,1)}, bf16[8192,128]{1,0:T(8,128)(2,1)S(1)}, u32[]{:S(2)}, u32[]{:S(2)}) collective-permute-start(bf16[8192,128]{1,0:T(8,128)(2,1)} %collective-permute-done.2), channel_id=1, source_target_pairs={{0,32},{32,0},{1,33},{33,1},{2,34},{34,2},{3,35},{35,3},{4,36},{36... | collective-permute-start | bytes 6291464 | tf_op jit(solution)/shard_map/ppermute | solution.py:15
  51.1 3.8 %copy-start.6 = (bf16[8192,128]{1,0:T(8,128)(2,1)S(1)}, bf16[8192,128]{1,0:T(8,128)(2,1)}, u32[]{:S(2)}) copy-start(bf16[8192,128]{1,0:T(8,128)(2,1)} %param.8) | copy-start | bytes 6291460
  51.2 14.9 %collective-permute-start.7 = (bf16[4096,128]{1,0:T(8,128)(2,1)S(1)}, bf16[4096,128]{1,0:T(8,128)(2,1)S(1)}, u32[]{:S(2)}, u32[]{:S(2)}) collective-permute-start(bf16[4096,128]{1,0:T(8,128)(2,1)S(1)} %get-tuple-element.25), channel_id=1, source_target_pairs={{0,64},{32,224},{64,128},{96,32},{128,192},{160,96},{192,0},{224,1... | collective-permute-start | bytes 3145736 | tf_op jit(solution)/shard_map/ppermute | solution.py:54
  52.6 24.7 %collective-permute-start.5 = (bf16[4096,128]{1,0:T(8,128)(2,1)S(1)}, bf16[4096,128]{1,0:T(8,128)(2,1)S(1)}, u32[]{:S(2)}, u32[]{:S(2)}) collective-permute-start(bf16[4096,128]{1,0:T(8,128)(2,1)S(1)} %get-tuple-element.24), channel_id=1, source_target_pairs={{0,64},{32,224},{64,128},{96,32},{128,192},{160,96},{192,0},{224,1... | collective-permute-start | bytes 3145736 | tf_op jit(solution)/shard_map/ppermute | solution.py:54
  54.2 27.8 %collective-permute-start.4 = (bf16[8192,128]{1,0:T(8,128)(2,1)}, bf16[8192,128]{1,0:T(8,128)(2,1)S(1)}, u32[]{:S(2)}, u32[]{:S(2)}) collective-permute-start(bf16[8192,128]{1,0:T(8,128)(2,1)} %collective-permute-done.1), channel_id=1, source_target_pairs={{0,32},{32,0},{1,33},{33,1},{2,34},{34,2},{3,35},{35,3},{4,36},{36... | collective-permute-start | bytes 6291464 | tf_op jit(solution)/shard_map/ppermute | solution.py:15
  66.0 20.6 %collective-permute-start.8 = (bf16[4096,128]{1,0:T(8,128)(2,1)S(1)}, bf16[4096,128]{1,0:T(8,128)(2,1)S(1)}, u32[]{:S(2)}, u32[]{:S(2)}) collective-permute-start(bf16[4096,128]{1,0:T(8,128)(2,1)S(1)} %collective-permute-done.7), channel_id=1, source_target_pairs={{0,32},{32,0},{1,33},{33,1},{2,34},{34,2},{3,35},{35,3},{4,36},{36... | collective-permute-start | bytes 3145736 | tf_op jit(solution)/shard_map/ppermute | solution.py:15
  77.3 10.7 %collective-permute-start.6 = (bf16[4096,128]{1,0:T(8,128)(2,1)S(1)}, bf16[4096,128]{1,0:T(8,128)(2,1)S(1)}, u32[]{:S(2)}, u32[]{:S(2)}) collective-permute-start(bf16[4096,128]{1,0:T(8,128)(2,1)S(1)} %collective-permute-done.5), channel_id=1, source_target_pairs={{0,32},{32,0},{1,33},{33,1},{2,34},{34,2},{3,35},{35,3},{4,36},{36... | collective-permute-start | bytes 3145736 | tf_op jit(solution)/shard_map/ppermute | solution.py:15
  102.9 17.6 %all-to-all-start.1 = ((f32[8,5,512]{2,1,0:T(8,128)}), f32[8,5,512]{2,1,0:T(8,128)S(1)}, u32[]{:S(2)}, u32[]{:S(2)}) async-start(f32[8,5,512]{2,1,0:T(8,128)} %broadcast_in_dim.51), calls=%async_computation.1 | async-start | bytes 262144 | tf_op jit(solution)/shard_map/all_to_all | solution.py:23
  111.3 9.2 %copy-start.3 = (f32[512]{0:T(512)S(1)}, f32[512]{0:T(512)}, u32[]{:S(2)}) copy-start(f32[512]{0:T(512)} %param.9) | copy-start | bytes 6148
  121.2 2.8 %copy-start.5 = (bf16[2048,1024]{1,0:T(8,128)(2,1)S(1)}, bf16[2048,1024]{1,0:T(8,128)(2,1)}, u32[]{:S(2)}) copy-start(bf16[2048,1024]{1,0:T(8,128)(2,1)} %param.7) | copy-start | bytes 12582916
  124.0 7.8 %copy-start.2 = (bf16[512,1024]{1,0:T(8,128)(2,1)}, bf16[512,1024]{1,0:T(8,128)(2,1)S(1)}, u32[]{:S(2)}) copy-start(bf16[512,1024]{1,0:T(8,128)(2,1)S(1)} %multiply_convert_fusion) | copy-start | bytes 3145732
  126.4 4.2 %copy-start = (bf16[512,2048]{0,1:T(8,128)(2,1)S(1)}, bf16[512,2048]{0,1:T(8,128)(2,1)}, u32[]{:S(2)}) copy-start(bf16[512,2048]{0,1:T(8,128)(2,1)} %copy.59) | copy-start | bytes 6291460
  127.3 16.7 %collective-permute-start.10 = (bf16[128,2048]{1,0:T(8,128)(2,1)}, bf16[128,2048]{1,0:T(8,128)(2,1)}, u32[]{:S(2)}, u32[]{:S(2)}) collective-permute-start(bf16[128,2048]{1,0:T(8,128)(2,1)} %get-tuple-element.23), channel_id=1, source_target_pairs={{0,2},{1,3},{2,0},{3,1},{4,6},{5,7},{6,4},{7,5},{8,10},{9,11},{10,... | collective-permute-start | bytes 1572872 | tf_op jit(solution)/shard_map/ppermute | solution.py:15
  128.3 22.1 %collective-permute-start.11 = (bf16[128,2048]{1,0:T(8,128)(2,1)S(1)}, bf16[128,2048]{1,0:T(8,128)(2,1)}, u32[]{:S(2)}, u32[]{:S(2)}) collective-permute-start(bf16[128,2048]{1,0:T(8,128)(2,1)S(1)} %get-tuple-element.22), channel_id=1, source_target_pairs={{0,3},{1,0},{2,1},{3,2},{4,7},{5,4},{6,5},{7,6},{8,11},{9,8},{10,9... | collective-permute-start | bytes 1572872 | tf_op jit(solution)/shard_map/ppermute | solution.py:15
  130.6 21.3 %collective-permute-start.9 = (bf16[128,2048]{1,0:T(8,128)(2,1)S(1)}, bf16[128,2048]{1,0:T(8,128)(2,1)}, u32[]{:S(2)}, u32[]{:S(2)}) collective-permute-start(bf16[128,2048]{1,0:T(8,128)(2,1)S(1)} %get-tuple-element.21), channel_id=1, source_target_pairs={{0,1},{1,2},{2,3},{3,0},{4,5},{5,6},{6,7},{7,4},{8,9},{9,10},{10,1... | collective-permute-start | bytes 1572872 | tf_op jit(solution)/shard_map/ppermute | solution.py:15
  134.4 44.1 %collective-permute-start.15 = (bf16[1024,1024]{1,0:T(8,128)(2,1)}, bf16[1024,1024]{1,0:T(8,128)(2,1)}, u32[]{:S(2)}, u32[]{:S(2)}) collective-permute-start(bf16[1024,1024]{1,0:T(8,128)(2,1)} %convolution_convert_fusion.1), channel_id=1, source_target_pairs={{0,32},{32,0},{1,33},{33,1},{2,34},{34,2},{3,35},{35,3},{4,36},{36... | collective-permute-start | bytes 6291464 | tf_op jit(solution)/shard_map/ppermute | solution.py:15
  174.9 19.8 %all-to-all-start.3 = ((bf16[8,16,2048]{2,1,0:T(8,128)(2,1)}), bf16[8,16,2048]{2,1,0:T(8,128)(2,1)S(1)}, u32[]{:S(2)}, u32[]{:S(2)}) async-start(bf16[8,16,2048]{2,1,0:T(8,128)(2,1)} %broadcast_in_dim.53), calls=%async_computation.3 | async-start | bytes 1048576 | tf_op jit(solution)/shard_map/all_to_all | solution.py:23
  183.1 15.1 %collective-permute-start.16 = (bf16[256,1024]{1,0:T(8,128)(2,1)}, bf16[256,1024]{1,0:T(8,128)(2,1)}, u32[]{:S(2)}, u32[]{:S(2)}) collective-permute-start(bf16[256,1024]{1,0:T(8,128)(2,1)} %get-tuple-element.16), channel_id=1, source_target_pairs={{0,64},{64,128},{128,192},{192,0},{1,65},{65,129},{129,193},{193,1... | collective-permute-start | bytes 1572872 | tf_op jit(solution)/shard_map/ppermute | solution.py:15
  184.4 16.6 %collective-permute-start.17 = (bf16[256,1024]{1,0:T(8,128)(2,1)}, bf16[256,1024]{1,0:T(8,128)(2,1)}, u32[]{:S(2)}, u32[]{:S(2)}) collective-permute-start(bf16[256,1024]{1,0:T(8,128)(2,1)} %get-tuple-element.18), channel_id=1, source_target_pairs={{0,128},{64,192},{128,0},{192,64},{1,129},{65,193},{129,1},{193,65... | collective-permute-start | bytes 1572872 | tf_op jit(solution)/shard_map/ppermute | solution.py:15
  187.1 22.4 %collective-permute-start.18 = (bf16[256,1024]{1,0:T(8,128)(2,1)S(1)}, bf16[256,1024]{1,0:T(8,128)(2,1)}, u32[]{:S(2)}, u32[]{:S(2)}) collective-permute-start(bf16[256,1024]{1,0:T(8,128)(2,1)S(1)} %get-tuple-element.17), channel_id=1, source_target_pairs={{0,192},{64,0},{128,64},{192,128},{1,193},{65,1},{129,65},{193,129... | collective-permute-start | bytes 1572872 | tf_op jit(solution)/shard_map/ppermute | solution.py:15
  194.7 17.3 %collective-permute-start.12 = (bf16[128,2048]{1,0:T(8,128)(2,1)S(1)}, bf16[128,2048]{1,0:T(8,128)(2,1)}, u32[]{:S(2)}, u32[]{:S(2)}) collective-permute-start(bf16[128,2048]{1,0:T(8,128)(2,1)S(1)} %bitcast.144), channel_id=1, source_target_pairs={{0,1},{32,35},{1,2},{33,32},{2,3},{34,33},{3,0},{35,34},{4,5},{36,... | collective-permute-start | bytes 1572872 | tf_op jit(solution)/shard_map/ppermute | solution.py:54
  194.7 18.4 %collective-permute-start.13 = (bf16[128,2048]{1,0:T(8,128)(2,1)S(1)}, bf16[128,2048]{1,0:T(8,128)(2,1)S(1)}, u32[]{:S(2)}, u32[]{:S(2)}) collective-permute-start(bf16[128,2048]{1,0:T(8,128)(2,1)S(1)} %bitcast.145), channel_id=1, source_target_pairs={{0,3},{32,33},{1,0},{33,34},{2,1},{34,35},{3,2},{35,32},{4,7},{36,... | collective-permute-start | bytes 1572872 | tf_op jit(solution)/shard_map/ppermute | solution.py:54
  212.0 10.6 %collective-permute-start.14 = (bf16[128,2048]{1,0:T(8,128)(2,1)}, bf16[128,2048]{1,0:T(8,128)(2,1)S(1)}, u32[]{:S(2)}, u32[]{:S(2)}) collective-permute-start(bf16[128,2048]{1,0:T(8,128)(2,1)} %collective-permute-done.12), channel_id=1, source_target_pairs={{0,1},{32,35},{1,2},{33,32},{2,3},{34,33},{3,0},{35,34},{4,5},{36,... | collective-permute-start | bytes 1572872 | tf_op jit(solution)/shard_map/ppermute | solution.py:54
  222.7 1.3 copy-start.1

commit v2 on v1

--- a/solution.py
+++ b/solution.py
@@ -59,26 +59,33 @@
     ring = lax.axis_size("x")
     half = own.shape[0] // 2
 
-    def product(hidden, mine, others):
-        pair = jnp.where(
+    def in_order(mine, others):
+        return jnp.where(
             core == 0,
             jnp.concatenate([mine, others], axis=1),
             jnp.concatenate([others, mine], axis=1),
         )
-        return dot(hidden, pair, ((1,), (0,)))
+
+    def product(hidden, *pieces):
+        return dot(hidden, in_order(*pieces), ((1,), (0,)))
 
     behind, ahead = turned(own, "x", 1), turned(own, "x", -1)
     far_top = turned(behind[:half], "x", 1)
     far_low = turned(behind[half:], "x", 1)
     own_part = product(hidden, own, shifted(own, "core", 1))
-    behind_part = product(hidden, behind, shifted(ahead, "core", 1))
-    ahead_part = product(hidden, ahead, shifted(behind, "core", 1))
+    behind_too, ahead_too = shifted(behind, "core", 1), shifted(ahead, "core", 1)
+    near = jnp.where(
+        core == 0,
+        jnp.concatenate([behind, ahead_too, ahead, behind_too], axis=1),
+        jnp.concatenate([ahead_too, behind, behind_too, ahead], axis=1),
+    )
+    near_part = dot(hidden, near, ((1,), (0,)))
     far_part = product(hidden[:, :half], far_top, shifted(far_top, "core", 1))
-    far_part = far_part + product(hidden[:, half:], far_low, shifted(far_low, "core", 1))
+    far_part = product(hidden[:, half:], far_low, shifted(far_low, "core", 1)) + far_part
     width = 2 * own.shape[1]
     back = jnp.where(core == 0, ring - 1, 1)
     logits = jnp.zeros((hidden.shape[0], ring * width), jnp.float32)
-    for step, part in ((0, own_part), (back, behind_part), (ring - back, ahead_part), (2, far_part)):
+    for step, part in ((0, own_part), (back, near_part[:, :width]), (ring - back, near_part[:, width:]), (2, far_part)):
         at = (place + step) % ring
         logits = lax.dynamic_update_slice(logits, part, (0, at * width))
     return logits
@@ -110,12 +117,14 @@
 
 def summed_head(draft_hidden, grad_logits):
     core = lax.axis_index("core")
-    tokens, width = draft_hidden.shape
+    width = draft_hidden.shape[1]
     ring = lax.axis_size("x")
-    strips = draft_hidden.reshape(tokens, ring, 2, width // (2 * ring))
+    block = width // (2 * ring)
 
     def strip(which):
-        return lax.dynamic_index_in_dim(strips, which, 2, keepdims=False).reshape(tokens, width // 2)
+        starts = [(2 * i + which) * block for i in range(ring)]
+        pieces = [lax.dynamic_slice_in_dim(draft_hidden, at, block, 1) for at in starts]
+        return jnp.concatenate(pieces, axis=1)
 
     away = dot(strip(1 - core), grad_logits, ((0,), (0,))).astype(jnp.bfloat16)
     away = shifted(away, "core", 1)

time: 225 us -> 227 us (level)
  waiting for transfers between devices: 107 us -> 119 us
  blocking collectives: 30.3 us -> 20.5 us
    all_to_all x2 -> x1, blocking collectives: 30.3 us -> 20.5 us  [exchanged(): return lax.all_to_all(pieces, axis, 0, 0, tiled=True)]
    all_to_all x2 -> x3, waiting for transfers between devices: 11.5 us -> 20.4 us  [exchanged(): return lax.all_to_all(pieces, axis, 0, 0, tiled=True)]
    unnamed x15 -> x24, local copies, waits for them, and re-layouts: 5.69 us -> 1.77 us
    all_to_all x2 -> x3, starting transfers between devices: 12 us -> 15.2 us  [exchanged(): return lax.all_to_all(pieces, axis, 0, 0, tiled=True)]
    ppermute x7, waiting for transfers between devices: 66.9 us -> 69.3 us  [turned(): return lax.ppermute(piece, axes, pairs)]
    dot_general x9 -> x8, matrix products: 31.7 us -> 30.2 us  [dot(): lax.dot_general(a, b, (contract, ((), ())), preferred_element_type=jnp.fl...]
  transfers between devices with their start and end apart: 21 -> 22, of which waited for: 11 -> 12; matrix products, arithmetic and copies ran while one was open for 19% -> 17% of each run, Pallas kernels for 0% -> 0%
where the time goes in v2:
time: 227 us; the launch traced here: 225 us
  waiting for transfers between devices  119 us (52%)
  starting transfers between devices  31.4 us (14%)
  matrix products  30.2 us (13%)
  blocking collectives  20.5 us (9%)
  local copies, waits for them, and re-layouts  12.4 us (5%)
  other arithmetic  10.4 us (5%)
    ppermute x7, waiting for transfers between devices, turned(): return lax.ppermute(piece, axes, pairs)  69.3 us
    dot_general x8, matrix products, dot(): lax.dot_general(a, b, (contract, ((), ())), preferred_element_type=jnp.fl...  30.2 us
    ppermute x12, waiting for transfers between devices, shifted(): return lax.ppermute(x, axis, [(i, (i + by) % n) for i in range(n)])  29.6 us
    all_to_all x1, blocking collectives, exchanged(): return lax.all_to_all(pieces, axis, 0, 0, tiled=True)  20.5 us
    all_to_all x3, waiting for transfers between devices, exchanged(): return lax.all_to_all(pieces, axis, 0, 0, tiled=True)  20.4 us
    all_to_all x3, starting transfers between devices, exchanged(): return lax.all_to_all(pieces, axis, 0, 0, tiled=True)  15.2 us
    ppermute x12, starting transfers between devices, shifted(): return lax.ppermute(x, axis, [(i, (i + by) % n) for i in range(n)])  8.4 us
    ppermute x7, starting transfers between devices, turned(): return lax.ppermute(piece, axes, pairs)  7.81 us
  transfers between devices with their start and end apart: 22, of which 12 were waited for; matrix products, arithmetic and copies ran while one was open for 17% of the time, Pallas kernels for 0%

profile of v2, /device:TPU:2, one launch (start us, length us, event | category | flops | bytes accessed | tf_op | source)
XLA Modules:
  0.0 225.2 jit_solution(9917427881106079850)
XLA Ops:
  0.6 1.6 collective-permute-start.1
  2.2 0.8 collective-permute-start.2
  3.0 0.0 collective-permute-start
  3.0 6.6 %fusion.100 = (f32[512]{0:T(512)S(1)}, f32[512,1024]{1,0:T(8,128)}) fusion(bf16[512,2048]{1,0:T(8,128)(2,1)} %param.5, bf16[2048,1024]{1,0:T(8,128)(2,1)} %param.7), kind=kOutput, calls=%fused_computation.141 | convolution fusion | flops 2148007424 | bytes 8390656 | tf_op jit(solution)/shard_map/dot_general | solution.py:19
  9.7 40.0 %collective-permute-done.1 = bf16[8192,128]{1,0:T(8,128)(2,1)} collective-permute-done((bf16[8192,128]{1,0:T(8,128)(2,1)}, bf16[8192,128]{1,0:T(8,128)(2,1)}, u32[]{:S(2)}, u32[]{:S(2)}) %collective-permute-start.1) | collective-permute-done | bytes 2097184 | tf_op jit(solution)/shard_map/ppermute | solution.py:54
  49.7 0.0 collective-permute-done.2
  49.7 0.5 collective-permute-start.3
  50.2 1.7 fusion.99
  51.9 0.0 copy-start.11
  51.9 0.5 collective-permute-start.7
  52.4 1.6 collective-permute-start.5
  54.1 0.2 broadcast_in_dim.49
  54.3 4.7 %fusion.41 = f32[512,1024]{1,0:T(8,128)S(1)} fusion(f32[512,1024]{1,0:T(8,128)S(1)} %broadcast_in_dim.49, s32[]{:T(128)S(6)} %select_n.166, bf16[512,8192]{1,0:T(8,128)(2,1)S(1)} %copy-done.9, bf16[8192,128]{1,0:T(8,128)(2,1)} %collective-permute-done, bf16[8192,128]{1,0:T(8,128)(2,1)S(1)} %copy-done.11, pred[]{:T(512)S(6)} %eq.25), kind=kOutput, calls=%fused_computation.52 | convolution fusion | flops 2166358016 | bytes 13107205 | tf_op jit(solution)/shard_map/dot_general | solution.py:19
  59.0 8.7 %collective-permute-done.7 = bf16[4096,128]{1,0:T(8,128)(2,1)S(1)} collective-permute-done((bf16[4096,128]{1,0:T(8,128)(2,1)S(1)}, bf16[4096,128]{1,0:T(8,128)(2,1)S(1)}, u32[]{:S(2)}, u32[]{:S(2)}) %collective-permute-start.7) | collective-permute-done | bytes 1048608 | tf_op jit(solution)/shard_map/ppermute | solution.py:54
  67.7 0.0 collective-permute-start.8
  67.7 11.2 %collective-permute-done.5 = bf16[4096,128]{1,0:T(8,128)(2,1)S(1)} collective-permute-done((bf16[4096,128]{1,0:T(8,128)(2,1)S(1)}, bf16[4096,128]{1,0:T(8,128)(2,1)S(1)}, u32[]{:S(2)}, u32[]{:S(2)}) %collective-permute-start.5) | collective-permute-done | bytes 1048608 | tf_op jit(solution)/shard_map/ppermute | solution.py:54
  78.9 0.0 collective-permute-start.6
  78.9 8.0 %fusion.39 = f32[512,512]{1,0:T(8,128)S(1)} fusion(bf16[512,8192]{1,0:T(8,128)(2,1)S(1)} %copy-done.9, bf16[8192,128]{1,0:T(8,128)(2,1)S(1)} %collective-permute-done.4, bf16[8192,128]{1,0:T(8,128)(2,1)} %collective-permute-done.2, bf16[8192,128]{1,0:T(8,128)(2,1)S(1)} %collective-permute-done.3, bf16[8192,128]{1,0:T(8,128)(2,1)} %collective-permute-done.1, ...), kind=kOutput, calls=%fused_computation.50 | convolution fusion | flops 4366270464 | bytes 17825792 | tf_op jit(solution)/shard_map/dot_general | solution.py:19
  87.0 0.1 slice_dynamic-update-slice_fusion.1
  87.1 1.3 fusion.21
  88.4 1.3 fusion.48
  89.7 0.2 reduce_max.55
  89.8 2.7 %multiply_reduce_fusion = (f32[512]{0:T(512)S(1)}, f32[512]{0:T(512)S(1)}, f32[512]{0:T(512)S(1)}) fusion(f32[512,1024]{1,0:T(8,128)S(1)} %fusion.48, f32[512,1024]{1,0:T(8,128)} %get-tuple-element.44, f32[512]{0:T(512)S(1)} %reduce_max.55, f32[512]{0:T(512)S(1)} %get-tuple-element.43), kind=kLoop, calls=%fused_computation.43 | loop fusion | flops 3668480 | bytes 4204544 | tf_op jit(solution)/shard_map/reduce_sum | solution.py:159
  92.6 0.6 broadcast_in_dim.50
  93.2 3.3 %all-to-all-start = ((f32[4,5,512]{2,1,0:T(8,128)}), f32[4,5,512]{2,1,0:T(8,128)S(1)}, u32[]{:S(2)}, u32[]{:S(2)}) async-start(f32[4,5,512]{2,1,0:T(8,128)} %broadcast_in_dim.50), calls=%async_computation | async-start | bytes 131072 | tf_op jit(solution)/shard_map/all_to_all | solution.py:23
  96.6 5.5 %all-to-all-done = f32[4,5,512]{2,1,0:T(8,128)S(1)} async-done(((f32[4,5,512]{2,1,0:T(8,128)}), f32[4,5,512]{2,1,0:T(8,128)S(1)}, u32[]{:S(2)}, u32[]{:S(2)}) %all-to-all-start) | async-done | bytes 40992 | tf_op jit(solution)/shard_map/all_to_all | solution.py:23
  102.2 0.7 broadcast_in_dim.51
  102.9 8.4 %all-to-all-start.1 = ((f32[8,5,512]{2,1,0:T(8,128)}), f32[8,5,512]{2,1,0:T(8,128)S(1)}, u32[]{:S(2)}, u32[]{:S(2)}) async-start(f32[8,5,512]{2,1,0:T(8,128)} %broadcast_in_dim.51), calls=%async_computation.1 | async-start | bytes 262144 | tf_op jit(solution)/shard_map/all_to_all | solution.py:23
  111.3 2.8 %constant_dynamic-slice_fusion.7 = (bf16[512,256]{1,0:T(8,128)(2,1)S(1)}, bf16[512,256]{1,0:T(8,128)(2,1)}, bf16[512,256]{1,0:T(8,128)(2,1)}, bf16[512,256]{1,0:...) fusion(bf16[512,2048]{1,0:T(8,128)(2,1)} %param.5, ...), kind=kLoop, calls=%fused_computation.126 | loop fusion | bytes 4194336 | tf_op jit(solution)/shard_map/dynamic_slice | solution.py:126
  114.1 6.3 %all-to-all-done.1 = f32[8,5,512]{2,1,0:T(8,128)S(1)} async-done(((f32[8,5,512]{2,1,0:T(8,128)}), f32[8,5,512]{2,1,0:T(8,128)S(1)}, u32[]{:S(2)}, u32[]{:S(2)}) %all-to-all-start.1) | async-done | bytes 81952 | tf_op jit(solution)/shard_map/all_to_all | solution.py:23
  120.4 0.1 slice_reduce_fusion.3
  120.6 0.6 add_multiply_fusion
  121.2 2.4 %multiply_convert_fusion = bf16[512,1024]{1,0:T(8,128)(2,1)S(1)} fusion(f32[512,1024]{1,0:T(8,128)S(1)} %fusion.48, f32[512,1024]{1,0:T(8,128)} %get-tuple-element.44, f32[512]{0:T(512)S(1)} %get-tuple-element.42, f32[512]{0:T(512)S(1)} %get-tuple-element.15, f32[512]{0:T(512)S(1)} %copy-done.8), kind=kLoop, calls=%fused_computation.42 | loop fusion | flops 2621440 | bytes 5249024 | tf_op jit(solution)/shard_map/convert_element_type | solution.py:169
  123.6 0.4 copy-done.10
  124.0 2.4 %convolution_convert_fusion = bf16[512,2048]{1,0:T(8,128)(2,1)S(1)} fusion(bf16[512,1024]{1,0:T(8,128)(2,1)S(1)} %multiply_convert_fusion, bf16[2048,1024]{1,0:T(8,128)(2,1)S(1)} %copy-done.10), kind=kOutput, calls=%fused_computation.29 | convolution fusion | flops 2148532224 | bytes 7340032 | tf_op jit(solution)/shard_map/dot_general | solution.py:19
  126.4 1.0 dynamic-slice_bitcast_fusion.5
  127.4 1.0 collective-permute-start.10
  128.3 2.2 collective-permute-start.11
  130.6 2.6 %convolution_convert_fusion.1 = bf16[1024,1024]{1,0:T(8,128)(2,1)} fusion(bf16[512,1024]{1,0:T(8,128)(2,1)S(1)} %multiply_convert_fusion, bf16[512,256]{1,0:T(8,128)(2,1)S(1)} %copy-done.6, bf16[512,256]{1,0:T(8,128)(2,1)S(1)} %copy-done.7, bf16[512,256]{1,0:T(8,128)(2,1)S(1)} %copy-done.4, bf16[512,256]{1,0:T(8,128)(2,1)S(1)} %copy-done.5), kind=kOutput, calls=%fused_computation.49 | convolution fusion | flops 1078984704 | bytes 4194304 | tf_op jit(solution)/shard_map/dot_general | solution.py:19
  133.2 10.8 %collective-permute-done.10 = bf16[128,2048]{1,0:T(8,128)(2,1)} collective-permute-done((bf16[128,2048]{1,0:T(8,128)(2,1)}, bf16[128,2048]{1,0:T(8,128)(2,1)}, u32[]{:S(2)}, u32[]{:S(2)}) %collective-permute-start.10) | collective-permute-done | bytes 524320 | tf_op jit(solution)/shard_map/ppermute | solution.py:15
  144.0 6.4 %collective-permute-done.11 = bf16[128,2048]{1,0:T(8,128)(2,1)} collective-permute-done((bf16[128,2048]{1,0:T(8,128)(2,1)S(1)}, bf16[128,2048]{1,0:T(8,128)(2,1)}, u32[]{:S(2)}, u32[]{:S(2)}) %collective-permute-start.11) | collective-permute-done | bytes 524320 | tf_op jit(solution)/shard_map/ppermute | solution.py:15
  150.4 1.5 collective-permute-done.9
  151.9 1.7 fusion.73
  153.6 20.5 %all_to_all.20 = bf16[8,16,2048]{2,1,0:T(8,128)(2,1)S(1)} all-to-all(bf16[8,16,2048]{2,1,0:T(8,128)(2,1)S(1)} %bitcast.134), channel_id=1, replica_groups=mesh['x'=4,'core'=2,'z'=8,'y'=4] {'z'}, dimensions={0} | all-to-all | bytes 1048576 | tf_op jit(solution)/shard_map/all_to_all | solution.py:23
  174.1 0.1 fusion.74
  174.2 0.8 broadcast_in_dim.53
  175.0 3.5 %all-to-all-start.3 = ((bf16[8,16,2048]{2,1,0:T(8,128)(2,1)}), bf16[8,16,2048]{2,1,0:T(8,128)(2,1)S(1)}, u32[]{:S(2)}, u32[]{:S(2)}) async-start(bf16[8,16,2048]{2,1,0:T(8,128)(2,1)} %broadcast_in_dim.53), calls=%async_computation.3 | async-start | bytes 1048576 | tf_op jit(solution)/shard_map/all_to_all | solution.py:23
  178.6 3.3 %add_convert_fusion = bf16[1024,1024]{1,0:T(8,128)(2,1)S(1)} fusion(bf16[1024,1024]{1,0:T(8,128)(2,1)} %collective-permute-done.15, bf16[512,1024]{1,0:T(8,128)(2,1)} %copy-done.1, bf16[512,256]{1,0:T(8,128)(2,1)S(1)} %copy-done.2, bf16[512,256]{1,0:T(8,128)(2,1)S(1)} %copy-done.3, bf16[512,256]{1,0:T(8,128)(2,1)} %get-tuple-element.24, ...), kind=kOutput, calls=%fused_computation.23 | convolution fusion | flops 1081081856 | bytes 6291456 | tf_op jit(solution)/shard_map/dot_general | solution.py:19
  181.9 1.1 dynamic-slice_bitcast_fusion.2
  183.0 0.8 collective-permute-start.16
  183.8 3.7 %collective-permute-start.17 = (bf16[256,1024]{1,0:T(8,128)(2,1)}, bf16[256,1024]{1,0:T(8,128)(2,1)}, u32[]{:S(2)}, u32[]{:S(2)}) collective-permute-start(bf16[256,1024]{1,0:T(8,128)(2,1)} %get-tuple-element.18), channel_id=1, source_target_pairs={{0,128},{64,192},{128,0},{192,64},{1,129},{65,193},{129,1},{193,65... | collective-permute-start | bytes 1572872 | tf_op jit(solution)/shard_map/ppermute | solution.py:15
  187.5 0.1 collective-permute-start.18
  187.7 8.6 %all-to-all-done.3 = bf16[8,16,2048]{2,1,0:T(8,128)(2,1)S(1)} async-done(((bf16[8,16,2048]{2,1,0:T(8,128)(2,1)}), bf16[8,16,2048]{2,1,0:T(8,128)(2,1)S(1)}, u32[]{:S(2)}, u32[]{:S(2)}) %all-to-all-start.3) | async-done | bytes 524320 | tf_op jit(solution)/shard_map/all_to_all | solution.py:23
  196.3 3.2 %collective-permute-start.13 = (bf16[128,2048]{1,0:T(8,128)(2,1)S(1)}, bf16[128,2048]{1,0:T(8,128)(2,1)S(1)}, u32[]{:S(2)}, u32[]{:S(2)}) collective-permute-start(bf16[128,2048]{1,0:T(8,128)(2,1)S(1)} %bitcast.132), channel_id=1, source_target_pairs={{0,3},{32,33},{1,0},{33,34},{2,1},{34,35},{3,2},{35,32},{4,7},{36,... | collective-permute-start | bytes 1572872 | tf_op jit(solution)/shard_map/ppermute | solution.py:54
  199.5 0.2 broadcast_in_dim.48
  199.7 0.1 bitcast_dynamic-update-slice_fusion.3
  199.8 0.8 collective-permute-done.17
  200.6 10.1 %collective-permute-done.18 = bf16[256,1024]{1,0:T(8,128)(2,1)} collective-permute-done((bf16[256,1024]{1,0:T(8,128)(2,1)S(1)}, bf16[256,1024]{1,0:T(8,128)(2,1)}, u32[]{:S(2)}, u32[]{:S(2)}) %collective-permute-start.18) | collective-permute-done | bytes 524320 | tf_op jit(solution)/shard_map/ppermute | solution.py:15
  210.8 2.5 %fusion.70 = bf16[256,1024]{1,0:T(8,128)(2,1)} fusion(bf16[256,1024]{1,0:T(8,128)(2,1)} %collective-permute-done.18, bf16[256,1024]{1,0:T(8,128)(2,1)} %collective-permute-done.17, bf16[256,1024]{1,0:T(8,128)(2,1)} %collective-permute-done.16, bf16[4,256,1024]{2,1,0:T(8,128)(2,1)S(1)} %bitcast.128, s32[]{:T(128)S(6)} %select_n.199), kind=kLoop, calls=%fused_computation.74 | loop fusion | flops 2097152 | bytes 2621444 | tf_op jit(solution)/shard_map/convert_element_type | solution.py:115
  213.3 1.1 bitcast_dynamic-update-slice_fusion.2
  214.4 0.1 bitcast_dynamic-update-slice_fusion.1
  214.5 9.4 %collective-permute-done.14 = bf16[128,2048]{1,0:T(8,128)(2,1)S(1)} collective-permute-done((bf16[128,2048]{1,0:T(8,128)(2,1)}, bf16[128,2048]{1,0:T(8,128)(2,1)S(1)}, u32[]{:S(2)}, u32[]{:S(2)}) %collective-permute-start.14) | collective-permute-done | bytes 524320 | tf_op jit(solution)/shard_map/ppermute | solution.py:54
  223.9 0.0 copy-start
  223.9 1.3 copy-done
  (42 shorter events, 0.4 us)
Async XLA Ops:
  0.6 49.1 %collective-permute-start.1 = (bf16[8192,128]{1,0:T(8,128)(2,1)}, bf16[8192,128]{1,0:T(8,128)(2,1)}, u32[]{:S(2)}, u32[]{:S(2)}) collective-permute-start(bf16[8192,128]{1,0:T(8,128)(2,1)} %param.8), channel_id=1, source_target_pairs={{0,64},{32,224},{64,128},{96,32},{128,192},{160,96},{192,0},{224,1... | collective-permute-start | bytes 6291464 | tf_op jit(solution)/shard_map/ppermute | solution.py:54
  2.2 47.5 %collective-permute-start.2 = (bf16[8192,128]{1,0:T(8,128)(2,1)}, bf16[8192,128]{1,0:T(8,128)(2,1)}, u32[]{:S(2)}, u32[]{:S(2)}) collective-permute-start(bf16[8192,128]{1,0:T(8,128)(2,1)} %param.8), channel_id=1, source_target_pairs={{0,192},{32,96},{64,0},{96,160},{128,64},{160,224},{192,128},{224,... | collective-permute-start | bytes 6291464 | tf_op jit(solution)/shard_map/ppermute | solution.py:54
  3.0 51.0 %collective-permute-start = (bf16[8192,128]{1,0:T(8,128)(2,1)}, bf16[8192,128]{1,0:T(8,128)(2,1)}, u32[]{:S(2)}, u32[]{:S(2)}) collective-permute-start(bf16[8192,128]{1,0:T(8,128)(2,1)} %param.8), channel_id=1, source_target_pairs={{0,32},{32,0},{1,33},{33,1},{2,34},{34,2},{3,35},{35,3},{4,36},{36... | collective-permute-start | bytes 6291464 | tf_op jit(solution)/shard_map/ppermute | solution.py:15
  3.0 51.3 %copy-start.9 = (bf16[512,8192]{1,0:T(8,128)(2,1)S(1)}, bf16[512,8192]{1,0:T(8,128)(2,1)}, u32[]{:S(2)}) copy-start(bf16[512,8192]{1,0:T(8,128)(2,1)} %param.6) | copy-start | bytes 25165828
  49.7 29.2 %collective-permute-start.4 = (bf16[8192,128]{1,0:T(8,128)(2,1)}, bf16[8192,128]{1,0:T(8,128)(2,1)S(1)}, u32[]{:S(2)}, u32[]{:S(2)}) collective-permute-start(bf16[8192,128]{1,0:T(8,128)(2,1)} %collective-permute-done.1), channel_id=1, source_target_pairs={{0,32},{32,0},{1,33},{33,1},{2,34},{34,2},{3,35},{35,3},{4,36},{36... | collective-permute-start | bytes 6291464 | tf_op jit(solution)/shard_map/ppermute | solution.py:15
  49.7 29.2 %collective-permute-start.3 = (bf16[8192,128]{1,0:T(8,128)(2,1)}, bf16[8192,128]{1,0:T(8,128)(2,1)S(1)}, u32[]{:S(2)}, u32[]{:S(2)}) collective-permute-start(bf16[8192,128]{1,0:T(8,128)(2,1)} %collective-permute-done.2), channel_id=1, source_target_pairs={{0,32},{32,0},{1,33},{33,1},{2,34},{34,2},{3,35},{35,3},{4,36},{36... | collective-permute-start | bytes 6291464 | tf_op jit(solution)/shard_map/ppermute | solution.py:15
  51.9 2.4 %copy-start.11 = (bf16[8192,128]{1,0:T(8,128)(2,1)S(1)}, bf16[8192,128]{1,0:T(8,128)(2,1)}, u32[]{:S(2)}) copy-start(bf16[8192,128]{1,0:T(8,128)(2,1)} %param.8) | copy-start | bytes 6291460
  51.9 15.8 %collective-permute-start.7 = (bf16[4096,128]{1,0:T(8,128)(2,1)S(1)}, bf16[4096,128]{1,0:T(8,128)(2,1)S(1)}, u32[]{:S(2)}, u32[]{:S(2)}) collective-permute-start(bf16[4096,128]{1,0:T(8,128)(2,1)S(1)} %get-tuple-element.31), channel_id=1, source_target_pairs={{0,64},{32,224},{64,128},{96,32},{128,192},{160,96},{192,0},{224,1... | collective-permute-start | bytes 3145736 | tf_op jit(solution)/shard_map/ppermute | solution.py:54
  52.4 26.5 %collective-permute-start.5 = (bf16[4096,128]{1,0:T(8,128)(2,1)S(1)}, bf16[4096,128]{1,0:T(8,128)(2,1)S(1)}, u32[]{:S(2)}, u32[]{:S(2)}) collective-permute-start(bf16[4096,128]{1,0:T(8,128)(2,1)S(1)} %get-tuple-element.30), channel_id=1, source_target_pairs={{0,64},{32,224},{64,128},{96,32},{128,192},{160,96},{192,0},{224,1... | collective-permute-start | bytes 3145736 | tf_op jit(solution)/shard_map/ppermute | solution.py:54
  67.7 19.4 %collective-permute-start.8 = (bf16[4096,128]{1,0:T(8,128)(2,1)S(1)}, bf16[4096,128]{1,0:T(8,128)(2,1)S(1)}, u32[]{:S(2)}, u32[]{:S(2)}) collective-permute-start(bf16[4096,128]{1,0:T(8,128)(2,1)S(1)} %collective-permute-done.7), channel_id=1, source_target_pairs={{0,32},{32,0},{1,33},{33,1},{2,34},{34,2},{3,35},{35,3},{4,36},{36... | collective-permute-start | bytes 3145736 | tf_op jit(solution)/shard_map/ppermute | solution.py:15
  78.9 9.4 %collective-permute-start.6 = (bf16[4096,128]{1,0:T(8,128)(2,1)S(1)}, bf16[4096,128]{1,0:T(8,128)(2,1)S(1)}, u32[]{:S(2)}, u32[]{:S(2)}) collective-permute-start(bf16[4096,128]{1,0:T(8,128)(2,1)S(1)} %collective-permute-done.5), channel_id=1, source_target_pairs={{0,32},{32,0},{1,33},{33,1},{2,34},{34,2},{3,35},{35,3},{4,36},{36... | collective-permute-start | bytes 3145736 | tf_op jit(solution)/shard_map/ppermute | solution.py:15
  93.2 8.9 %all-to-all-start = ((f32[4,5,512]{2,1,0:T(8,128)}), f32[4,5,512]{2,1,0:T(8,128)S(1)}, u32[]{:S(2)}, u32[]{:S(2)}) async-start(f32[4,5,512]{2,1,0:T(8,128)} %broadcast_in_dim.50), calls=%async_computation | async-start | bytes 131072 | tf_op jit(solution)/shard_map/all_to_all | solution.py:23
  102.9 17.5 %all-to-all-start.1 = ((f32[8,5,512]{2,1,0:T(8,128)}), f32[8,5,512]{2,1,0:T(8,128)S(1)}, u32[]{:S(2)}, u32[]{:S(2)}) async-start(f32[8,5,512]{2,1,0:T(8,128)} %broadcast_in_dim.51), calls=%async_computation.1 | async-start | bytes 262144 | tf_op jit(solution)/shard_map/all_to_all | solution.py:23
  111.3 9.2 %copy-start.8 = (f32[512]{0:T(512)S(1)}, f32[512]{0:T(512)}, u32[]{:S(2)}) copy-start(f32[512]{0:T(512)} %param.9) | copy-start | bytes 6148
  121.2 2.8 %copy-start.10 = (bf16[2048,1024]{1,0:T(8,128)(2,1)S(1)}, bf16[2048,1024]{1,0:T(8,128)(2,1)}, u32[]{:S(2)}) copy-start(bf16[2048,1024]{1,0:T(8,128)(2,1)} %param.7) | copy-start | bytes 12582916
  124.0 6.6 %copy-start.1 = (bf16[512,1024]{1,0:T(8,128)(2,1)}, bf16[512,1024]{1,0:T(8,128)(2,1)S(1)}, u32[]{:S(2)}) copy-start(bf16[512,1024]{1,0:T(8,128)(2,1)S(1)} %multiply_convert_fusion) | copy-start | bytes 3145732
  126.4 4.2 %copy-start.4 = (bf16[512,256]{1,0:T(8,128)(2,1)S(1)}, bf16[512,256]{1,0:T(8,128)(2,1)}, u32[]{:S(2)}) copy-start(bf16[512,256]{1,0:T(8,128)(2,1)} %get-tuple-element.20) | copy-start | bytes 786436
  126.4 4.2 %copy-start.5 = (bf16[512,256]{1,0:T(8,128)(2,1)S(1)}, bf16[512,256]{1,0:T(8,128)(2,1)}, u32[]{:S(2)}) copy-start(bf16[512,256]{1,0:T(8,128)(2,1)} %get-tuple-element.21) | copy-start | bytes 786436
  126.4 4.2 %copy-start.6 = (bf16[512,256]{1,0:T(8,128)(2,1)S(1)}, bf16[512,256]{1,0:T(8,128)(2,1)}, u32[]{:S(2)}) copy-start(bf16[512,256]{1,0:T(8,128)(2,1)} %get-tuple-element.25) | copy-start | bytes 786436
  126.4 4.2 %copy-start.7 = (bf16[512,256]{1,0:T(8,128)(2,1)S(1)}, bf16[512,256]{1,0:T(8,128)(2,1)}, u32[]{:S(2)}) copy-start(bf16[512,256]{1,0:T(8,128)(2,1)} %get-tuple-element.26) | copy-start | bytes 786436
  127.4 16.7 %collective-permute-start.10 = (bf16[128,2048]{1,0:T(8,128)(2,1)}, bf16[128,2048]{1,0:T(8,128)(2,1)}, u32[]{:S(2)}, u32[]{:S(2)}) collective-permute-start(bf16[128,2048]{1,0:T(8,128)(2,1)} %get-tuple-element.29), channel_id=1, source_target_pairs={{0,2},{1,3},{2,0},{3,1},{4,6},{5,7},{6,4},{7,5},{8,10},{9,11},{10,... | collective-permute-start | bytes 1572872 | tf_op jit(solution)/shard_map/ppermute | solution.py:15
  128.3 22.1 %collective-permute-start.11 = (bf16[128,2048]{1,0:T(8,128)(2,1)S(1)}, bf16[128,2048]{1,0:T(8,128)(2,1)}, u32[]{:S(2)}, u32[]{:S(2)}) collective-permute-start(bf16[128,2048]{1,0:T(8,128)(2,1)S(1)} %get-tuple-element.28), channel_id=1, source_target_pairs={{0,3},{1,0},{2,1},{3,2},{4,7},{5,4},{6,5},{7,6},{8,11},{9,8},{10,9... | collective-permute-start | bytes 1572872 | tf_op jit(solution)/shard_map/ppermute | solution.py:15
  130.6 21.3 %collective-permute-start.9 = (bf16[128,2048]{1,0:T(8,128)(2,1)S(1)}, bf16[128,2048]{1,0:T(8,128)(2,1)}, u32[]{:S(2)}, u32[]{:S(2)}) collective-permute-start(bf16[128,2048]{1,0:T(8,128)(2,1)S(1)} %get-tuple-element.27), channel_id=1, source_target_pairs={{0,1},{1,2},{2,3},{3,0},{4,5},{5,6},{6,7},{7,4},{8,9},{9,10},{10,1... | collective-permute-start | bytes 1572872 | tf_op jit(solution)/shard_map/ppermute | solution.py:15
  133.2 45.3 %collective-permute-start.15 = (bf16[1024,1024]{1,0:T(8,128)(2,1)}, bf16[1024,1024]{1,0:T(8,128)(2,1)}, u32[]{:S(2)}, u32[]{:S(2)}) collective-permute-start(bf16[1024,1024]{1,0:T(8,128)(2,1)} %convolution_convert_fusion.1), channel_id=1, source_target_pairs={{0,32},{32,0},{1,33},{33,1},{2,34},{34,2},{3,35},{35,3},{4,36},{36... | collective-permute-start | bytes 6291464 | tf_op jit(solution)/shard_map/ppermute | solution.py:15
  153.6 25.0 %copy-start.2 = (bf16[512,256]{1,0:T(8,128)(2,1)S(1)}, bf16[512,256]{1,0:T(8,128)(2,1)}, u32[]{:S(2)}) copy-start(bf16[512,256]{1,0:T(8,128)(2,1)} %get-tuple-element.22) | copy-start | bytes 786436
  153.6 25.0 %copy-start.3 = (bf16[512,256]{1,0:T(8,128)(2,1)S(1)}, bf16[512,256]{1,0:T(8,128)(2,1)}, u32[]{:S(2)}) copy-start(bf16[512,256]{1,0:T(8,128)(2,1)} %get-tuple-element.23) | copy-start | bytes 786436
  175.0 21.2 %all-to-all-start.3 = ((bf16[8,16,2048]{2,1,0:T(8,128)(2,1)}), bf16[8,16,2048]{2,1,0:T(8,128)(2,1)S(1)}, u32[]{:S(2)}, u32[]{:S(2)}) async-start(bf16[8,16,2048]{2,1,0:T(8,128)(2,1)} %broadcast_in_dim.53), calls=%async_computation.3 | async-start | bytes 1048576 | tf_op jit(solution)/shard_map/all_to_all | solution.py:23
  183.0 16.8 %collective-permute-start.16 = (bf16[256,1024]{1,0:T(8,128)(2,1)}, bf16[256,1024]{1,0:T(8,128)(2,1)}, u32[]{:S(2)}, u32[]{:S(2)}) collective-permute-start(bf16[256,1024]{1,0:T(8,128)(2,1)} %get-tuple-element.16), channel_id=1, source_target_pairs={{0,64},{64,128},{128,192},{192,0},{1,65},{65,129},{129,193},{193,1... | collective-permute-start | bytes 1572872 | tf_op jit(solution)/shard_map/ppermute | solution.py:15
  183.8 16.9 %collective-permute-start.17 = (bf16[256,1024]{1,0:T(8,128)(2,1)}, bf16[256,1024]{1,0:T(8,128)(2,1)}, u32[]{:S(2)}, u32[]{:S(2)}) collective-permute-start(bf16[256,1024]{1,0:T(8,128)(2,1)} %get-tuple-element.18), channel_id=1, source_target_pairs={{0,128},{64,192},{128,0},{192,64},{1,129},{65,193},{129,1},{193,65... | collective-permute-start | bytes 1572872 | tf_op jit(solution)/shard_map/ppermute | solution.py:15
  187.5 23.2 %collective-permute-start.18 = (bf16[256,1024]{1,0:T(8,128)(2,1)S(1)}, bf16[256,1024]{1,0:T(8,128)(2,1)}, u32[]{:S(2)}, u32[]{:S(2)}) collective-permute-start(bf16[256,1024]{1,0:T(8,128)(2,1)S(1)} %get-tuple-element.17), channel_id=1, source_target_pairs={{0,192},{64,0},{128,64},{192,128},{1,193},{65,1},{129,65},{193,129... | collective-permute-start | bytes 1572872 | tf_op jit(solution)/shard_map/ppermute | solution.py:15
  196.3 17.0 %collective-permute-start.12 = (bf16[128,2048]{1,0:T(8,128)(2,1)S(1)}, bf16[128,2048]{1,0:T(8,128)(2,1)}, u32[]{:S(2)}, u32[]{:S(2)}) collective-permute-start(bf16[128,2048]{1,0:T(8,128)(2,1)S(1)} %bitcast.131), channel_id=1, source_target_pairs={{0,1},{32,35},{1,2},{33,32},{2,3},{34,33},{3,0},{35,34},{4,5},{36,... | collective-permute-start | bytes 1572872 | tf_op jit(solution)/shard_map/ppermute | solution.py:54
  196.3 18.1 %collective-permute-start.13 = (bf16[128,2048]{1,0:T(8,128)(2,1)S(1)}, bf16[128,2048]{1,0:T(8,128)(2,1)S(1)}, u32[]{:S(2)}, u32[]{:S(2)}) collective-permute-start(bf16[128,2048]{1,0:T(8,128)(2,1)S(1)} %bitcast.132), channel_id=1, source_target_pairs={{0,3},{32,33},{1,0},{33,34},{2,1},{34,35},{3,2},{35,32},{4,7},{36,... | collective-permute-start | bytes 1572872 | tf_op jit(solution)/shard_map/ppermute | solution.py:54
  213.3 10.6 %collective-permute-start.14 = (bf16[128,2048]{1,0:T(8,128)(2,1)}, bf16[128,2048]{1,0:T(8,128)(2,1)S(1)}, u32[]{:S(2)}, u32[]{:S(2)}) collective-permute-start(bf16[128,2048]{1,0:T(8,128)(2,1)} %collective-permute-done.12), channel_id=1, source_target_pairs={{0,1},{32,35},{1,2},{33,32},{2,3},{34,33},{3,0},{35,34},{4,5},{36,... | collective-permute-start | bytes 1572872 | tf_op jit(solution)/shard_map/ppermute | solution.py:54
  223.9 1.3 copy-start

commit v3 on v2

--- a/solution.py
+++ b/solution.py
@@ -57,7 +57,7 @@
 def teacher_product(hidden, own):
     place, core = lax.axis_index("x"), lax.axis_index("core")
     ring = lax.axis_size("x")
-    half = own.shape[0] // 2
+    half = own.shape[0] * 3 // 4
 
     def in_order(mine, others):
         return jnp.where(
@@ -134,10 +134,22 @@
     return added(pieces)
 
 
+def summed_ring(pieces, axis):
+    n, place, core = lax.axis_size(axis), lax.axis_index(axis), lax.axis_index("core")
+    back = jnp.where(core == 0, n - 1, 1)
+
+    def piece(step):
+        return lax.dynamic_index_in_dim(pieces, (place + step) % n, 0, keepdims=False)
+
+    far = turned(piece(2), axis, 1)
+    other = turned(piece(back), axis, -1)
+    on = turned(added([far, piece(n - back)]), axis, 1)
+    return added([piece(0), other, on])
+
+
 def summed(part):
     n, m = lax.axis_size("y"), lax.axis_size("z")
-    pieces = swapped(part.reshape(n, -1, part.shape[1]), "y")
-    rows = added(pieces)
+    rows = summed_ring(part.reshape(n, -1, part.shape[1]), "y")
     pieces = exchanged(rows.reshape(m, -1, rows.shape[1]), "z")
     block = added(pieces)
     rows = sent_to_all(block, "z").reshape(rows.shape)

time: 227 us -> 229 us (level)
  blocking collectives: 20.5 us -> 8.65 us
  matrix products: 30.2 us -> 38.6 us
    ppermute x12 -> x9, waiting for transfers between devices: 29.6 us -> 10.3 us  [shifted(): return lax.ppermute(x, axis, [(i, (i + by) % n) for i in range(n)])]
    ppermute x7 -> x10, waiting for transfers between devices: 69.3 us -> 83.2 us  [turned(): return lax.ppermute(piece, axes, pairs)]
    all_to_all x1, blocking collectives: 20.5 us -> 8.65 us  [exchanged(): return lax.all_to_all(pieces, axis, 0, 0, tiled=True)]
    dot_general x8, matrix products: 30.2 us -> 38.6 us  [dot(): lax.dot_general(a, b, (contract, ((), ())), preferred_element_type=jnp.fl...]
    all_to_all x3, waiting for transfers between devices: 20.4 us -> 26.7 us  [exchanged(): return lax.all_to_all(pieces, axis, 0, 0, tiled=True)]
    ppermute x7 -> x10, starting transfers between devices: 7.81 us -> 12 us  [turned(): return lax.ppermute(piece, axes, pairs)]
    ppermute x12 -> x9, starting transfers between devices: 8.4 us -> 5.37 us  [shifted(): return lax.ppermute(x, axis, [(i, (i + by) % n) for i in range(n)])]
    slice x0 -> x1, local copies, waits for them, and re-layouts: none -> 2.73 us  [teacher_product(): far_top = turned(behind[:half], 'x', 1)]
  transfers between devices with their start and end apart: 22 -> 22, of which waited for: 12 -> 12; matrix products, arithmetic and copies ran while one was open for 17% -> 22% of each run, Pallas kernels for 0% -> 0%
where the time goes in v3:
time: 229 us; the launch traced here: 227 us
  waiting for transfers between devices  120 us (52%)
  matrix products  38.6 us (17%)
  starting transfers between devices  32.9 us (14%)
  local copies, waits for them, and re-layouts  13.5 us (6%)
  other arithmetic  12.1 us (5%)
  blocking collectives  8.65 us (4%)
    ppermute x10, waiting for transfers between devices, turned(): return lax.ppermute(piece, axes, pairs)  83.2 us
    dot_general x8, matrix products, dot(): lax.dot_general(a, b, (contract, ((), ())), preferred_element_type=jnp.fl...  38.6 us
    all_to_all x3, waiting for transfers between devices, exchanged(): return lax.all_to_all(pieces, axis, 0, 0, tiled=True)  26.7 us
    all_to_all x3, starting transfers between devices, exchanged(): return lax.all_to_all(pieces, axis, 0, 0, tiled=True)  15.6 us
    ppermute x10, starting transfers between devices, turned(): return lax.ppermute(piece, axes, pairs)  12 us
    ppermute x9, waiting for transfers between devices, shifted(): return lax.ppermute(x, axis, [(i, (i + by) % n) for i in range(n)])  10.3 us
    all_to_all x1, blocking collectives, exchanged(): return lax.all_to_all(pieces, axis, 0, 0, tiled=True)  8.65 us
    convert_element_type x3, other arithmetic, added(): sum((piece.astype(jnp.float32) for piece in pieces)).astype(jnp.bfloat16)  5.91 us
  transfers between devices with their start and end apart: 22, of which 12 were waited for; matrix products, arithmetic and copies ran while one was open for 22% of the time, Pallas kernels for 0%

profile of v3, /device:TPU:2, one launch (start us, length us, event | category | flops | bytes accessed | tf_op | source)
XLA Modules:
  0.0 226.8 jit_solution(11459161135000880417)
XLA Ops:
  0.6 0.0 copy-start
  0.6 1.6 collective-permute-start.1
  2.2 0.8 collective-permute-start.2
  3.1 46.6 %collective-permute-done.1 = bf16[8192,128]{1,0:T(8,128)(2,1)} collective-permute-done((bf16[8192,128]{1,0:T(8,128)(2,1)}, bf16[8192,128]{1,0:T(8,128)(2,1)}, u32[]{:S(2)}, u32[]{:S(2)}) %collective-permute-start.1) | collective-permute-done | bytes 2097184 | tf_op jit(solution)/shard_map/ppermute | solution.py:54
  49.7 2.7 %slice.71 = bf16[6144,128]{1,0:T(8,128)(2,1)} slice(bf16[8192,128]{1,0:T(8,128)(2,1)} %collective-permute-done.1), slice={[0:6144], [0:128]} | slice | bytes 3145728 | tf_op jit(solution)/shard_map/slice | solution.py:73
  52.4 0.4 collective-permute-start.7
  52.9 0.5 collective-permute-start.3
  53.4 5.9 %fusion.99 = (f32[512]{0:T(512)S(1)}, f32[512,1024]{1,0:T(8,128)}) fusion(bf16[512,2048]{1,0:T(8,128)(2,1)S(1)} %copy-done, bf16[2048,1024]{1,0:T(8,128)(2,1)} %param.7), kind=kOutput, calls=%fused_computation.140 | convolution fusion | flops 2148007424 | bytes 8390656 | tf_op jit(solution)/shard_map/dot_general | solution.py:19
  59.3 1.1 slice.70
  60.3 1.6 collective-permute-start.5
  61.9 0.2 broadcast_in_dim.49
  62.2 0.0 slice-start.1
  62.2 8.4 %fusion.44 = f32[512,1024]{1,0:T(8,128)S(1)} fusion(f32[512,1024]{1,0:T(8,128)S(1)} %broadcast_in_dim.49, s32[]{:T(128)S(6)} %select_n.163, bf16[512,8192]{1,0:T(8,128)(2,1)} %param.6, bf16[8192,128]{1,0:T(8,128)(2,1)} %collective-permute-done, bf16[8192,128]{1,0:T(8,128)(2,1)} %param.8, pred[]{:T(512)S(6)} %eq.26), kind=kOutput, calls=%fused_computation.48 | convolution fusion | flops 2166358016 | bytes 13107205 | tf_op jit(solution)/shard_map/dot_general | solution.py:19
  70.6 9.0 %collective-permute-done.5 = bf16[2048,128]{1,0:T(8,128)(2,1)S(1)} collective-permute-done((bf16[2048,128]{1,0:T(8,128)(2,1)S(1)}, bf16[2048,128]{1,0:T(8,128)(2,1)S(1)}, u32[]{:S(2)}, u32[]{:S(2)}) %collective-permute-start.5) | collective-permute-done | bytes 524320 | tf_op jit(solution)/shard_map/ppermute | solution.py:54
  79.6 0.5 collective-permute-start.8
  80.1 11.6 %fusion.33 = f32[512,512]{1,0:T(8,128)S(1)} fusion(bf16[512,8192]{1,0:T(8,128)(2,1)S(1)} %bitcast.147, bf16[8192,128]{1,0:T(8,128)(2,1)} %collective-permute-done.4, bf16[8192,128]{1,0:T(8,128)(2,1)} %collective-permute-done.2, bf16[8192,128]{1,0:T(8,128)(2,1)} %collective-permute-done.3, bf16[8192,128]{1,0:T(8,128)(2,1)} %collective-permute-done.1, ...), kind=kOutput, calls=%fused_computation.43 | convolution fusion | flops 4366270464 | bytes 17825792 | tf_op jit(solution)/shard_map/dot_general | solution.py:19
  91.7 0.1 slice_dynamic-update-slice_fusion.1
  91.8 3.8 %fusion.15 = f32[256,512]{0,1:T(8,128)S(1)} fusion(bf16[512,8192]{1,0:T(8,128)(2,1)S(1)} %bitcast.147, bf16[6144,128]{1,0:T(8,128)(2,1)S(1)} %collective-permute-done.8, bf16[6144,128]{1,0:T(8,128)(2,1)} %collective-permute-done.7, pred[]{:T(512)S(6)} %eq.26), kind=kOutput, calls=%fused_computation.16 | convolution fusion | flops 1624768512 | bytes 9961473 | tf_op jit(solution)/shard_map/dot_general | solution.py:19
  95.6 0.7 fusion.40
  96.4 0.2 reduce_max.55
  96.5 2.7 %multiply_reduce_fusion = (f32[512]{0:T(512)S(1)}, f32[512]{0:T(512)S(1)}, f32[512]{0:T(512)S(1)}) fusion(f32[512,1024]{1,0:T(8,128)S(1)} %fusion.40, f32[512,1024]{1,0:T(8,128)} %get-tuple-element.41, f32[512]{0:T(512)S(1)} %reduce_max.55, f32[512]{0:T(512)S(1)} %get-tuple-element.40), kind=kLoop, calls=%fused_computation.36 | loop fusion | flops 3668480 | bytes 4204544 | tf_op jit(solution)/shard_map/reduce_sum | solution.py:171
  99.3 8.7 %all_to_all.20 = f32[4,5,512]{2,1,0:T(8,128)S(1)} all-to-all(f32[4,5,512]{2,1,0:T(8,128)S(1)} %broadcast_in_dim.50), channel_id=1, replica_groups=mesh['x'=4,'core'=2,'z'=8,'y'=4] {'y'}, dimensions={0} | all-to-all | bytes 81920 | tf_op jit(solution)/shard_map/all_to_all | solution.py:23
  108.1 0.7 broadcast_in_dim.51
  108.7 8.5 %all-to-all-start.1 = ((f32[8,5,512]{2,1,0:T(8,128)}), f32[8,5,512]{2,1,0:T(8,128)S(1)}, u32[]{:S(2)}, u32[]{:S(2)}) async-start(f32[8,5,512]{2,1,0:T(8,128)} %broadcast_in_dim.51), calls=%async_computation.1 | async-start | bytes 262144 | tf_op jit(solution)/shard_map/all_to_all | solution.py:23
  117.2 9.1 %all-to-all-done.1 = f32[8,5,512]{2,1,0:T(8,128)S(1)} async-done(((f32[8,5,512]{2,1,0:T(8,128)}), f32[8,5,512]{2,1,0:T(8,128)S(1)}, u32[]{:S(2)}, u32[]{:S(2)}) %all-to-all-start.1) | async-done | bytes 81952 | tf_op jit(solution)/shard_map/all_to_all | solution.py:23
  126.3 0.1 slice_reduce_fusion.3
  126.4 0.6 add_multiply_fusion
  127.0 2.4 %multiply_convert_fusion = bf16[512,1024]{1,0:T(8,128)(2,1)S(1)} fusion(f32[512,1024]{1,0:T(8,128)S(1)} %fusion.40, f32[512,1024]{1,0:T(8,128)} %get-tuple-element.41, f32[512]{0:T(512)S(1)} %get-tuple-element.39, f32[512]{0:T(512)S(1)} %get-tuple-element.15, f32[512]{0:T(512)S(1)} %copy-done.7), kind=kLoop, calls=%fused_computation.35 | loop fusion | flops 2621440 | bytes 5249024 | tf_op jit(solution)/shard_map/convert_element_type | solution.py:181
  129.4 0.4 copy-done.8
  129.8 2.4 %convolution_convert_fusion = bf16[512,2048]{1,0:T(8,128)(2,1)S(1)} fusion(bf16[512,1024]{1,0:T(8,128)(2,1)S(1)} %multiply_convert_fusion, bf16[2048,1024]{1,0:T(8,128)(2,1)S(1)} %copy-done.8), kind=kOutput, calls=%fused_computation.34 | convolution fusion | flops 2148532224 | bytes 7340032 | tf_op jit(solution)/shard_map/dot_general | solution.py:19
  132.3 1.3 copy-done.3
  133.6 1.0 dynamic-slice_bitcast_fusion.4
  134.6 0.6 collective-permute-start.10
  135.2 1.1 constant_dynamic-slice_fusion.7
  136.2 2.7 %collective-permute-start.9 = (bf16[128,2048]{1,0:T(8,128)(2,1)}, bf16[128,2048]{1,0:T(8,128)(2,1)S(1)}, u32[]{:S(2)}, u32[]{:S(2)}) collective-permute-start(bf16[128,2048]{1,0:T(8,128)(2,1)} %get-tuple-element.27), channel_id=1, source_target_pairs={{0,3},{32,33},{1,0},{33,34},{2,1},{34,35},{3,2},{35,32},{4,7},{36,... | collective-permute-start | bytes 1572872 | tf_op jit(solution)/shard_map/ppermute | solution.py:54
  138.9 10.3 %collective-permute-done.10 = bf16[128,2048]{1,0:T(8,128)(2,1)} collective-permute-done((bf16[128,2048]{1,0:T(8,128)(2,1)}, bf16[128,2048]{1,0:T(8,128)(2,1)}, u32[]{:S(2)}, u32[]{:S(2)}) %collective-permute-start.10) | collective-permute-done | bytes 524320 | tf_op jit(solution)/shard_map/ppermute | solution.py:54
  149.2 1.3 fusion.70
  150.5 0.1 collective-permute-start.11
  150.6 2.6 %convolution_convert_fusion.1 = bf16[1024,1024]{1,0:T(8,128)(2,1)} fusion(bf16[512,1024]{1,0:T(8,128)(2,1)S(1)} %multiply_convert_fusion, bf16[512,256]{1,0:T(8,128)(2,1)S(1)} %get-tuple-element.25, bf16[512,256]{1,0:T(8,128)(2,1)S(1)} %get-tuple-element.26, bf16[512,256]{1,0:T(8,128)(2,1)S(1)} %get-tuple-element.20, bf16[512,256]{1,0:T(8,128)(2,1)S(1)} %get-tuple-element.21), kind=kOutput, calls=%fused_computation.42 | convolution fusion | flops 1078984704 | bytes 4194304 | tf_op jit(solution)/shard_map/dot_general | solution.py:19
  153.2 7.8 %collective-permute-done.11 = bf16[128,2048]{1,0:T(8,128)(2,1)S(1)} collective-permute-done((bf16[128,2048]{1,0:T(8,128)(2,1)S(1)}, bf16[128,2048]{1,0:T(8,128)(2,1)S(1)}, u32[]{:S(2)}, u32[]{:S(2)}) %collective-permute-start.11) | collective-permute-done | bytes 524320 | tf_op jit(solution)/shard_map/ppermute | solution.py:54
  161.0 2.1 fusion.72
  163.1 3.6 %all-to-all-start.2 = ((bf16[8,16,2048]{2,1,0:T(8,128)(2,1)}), bf16[8,16,2048]{2,1,0:T(8,128)(2,1)S(1)}, u32[]{:S(2)}, u32[]{:S(2)}) async-start(bf16[8,16,2048]{2,1,0:T(8,128)(2,1)} %bitcast.24), calls=%async_computation.2 | async-start | bytes 1048576 | tf_op jit(solution)/shard_map/all_to_all | solution.py:23
  166.7 13.2 %all-to-all-done.2 = bf16[8,16,2048]{2,1,0:T(8,128)(2,1)S(1)} async-done(((bf16[8,16,2048]{2,1,0:T(8,128)(2,1)}), bf16[8,16,2048]{2,1,0:T(8,128)(2,1)S(1)}, u32[]{:S(2)}, u32[]{:S(2)}) %all-to-all-start.2) | async-done | bytes 524320 | tf_op jit(solution)/shard_map/all_to_all | solution.py:23
  179.9 0.1 fusion.74
  180.0 0.8 broadcast_in_dim.53
  180.8 3.5 %all-to-all-start.3 = ((bf16[8,16,2048]{2,1,0:T(8,128)(2,1)}), bf16[8,16,2048]{2,1,0:T(8,128)(2,1)S(1)}, u32[]{:S(2)}, u32[]{:S(2)}) async-start(bf16[8,16,2048]{2,1,0:T(8,128)(2,1)} %broadcast_in_dim.53), calls=%async_computation.3 | async-start | bytes 1048576 | tf_op jit(solution)/shard_map/all_to_all | solution.py:23
  184.4 3.3 %add_convert_fusion = bf16[1024,1024]{1,0:T(8,128)(2,1)S(1)} fusion(bf16[1024,1024]{1,0:T(8,128)(2,1)} %collective-permute-done.15, bf16[512,1024]{1,0:T(8,128)(2,1)} %copy-done.4, bf16[512,256]{1,0:T(8,128)(2,1)S(1)} %copy-done.5, bf16[512,256]{1,0:T(8,128)(2,1)S(1)} %copy-done.6, bf16[512,256]{1,0:T(8,128)(2,1)} %get-tuple-element.24, ...), kind=kOutput, calls=%fused_computation.25 | convolution fusion | flops 1081081856 | bytes 6291456 | tf_op jit(solution)/shard_map/dot_general | solution.py:19
  187.6 1.1 dynamic-slice_bitcast_fusion.2
  188.8 0.8 collective-permute-start.16
  189.6 3.1 %collective-permute-start.17 = (bf16[256,1024]{1,0:T(8,128)(2,1)}, bf16[256,1024]{1,0:T(8,128)(2,1)}, u32[]{:S(2)}, u32[]{:S(2)}) collective-permute-start(bf16[256,1024]{1,0:T(8,128)(2,1)} %get-tuple-element.18), channel_id=1, source_target_pairs={{0,128},{64,192},{128,0},{192,64},{1,129},{65,193},{129,1},{193,65... | collective-permute-start | bytes 1572872 | tf_op jit(solution)/shard_map/ppermute | solution.py:15
  192.6 0.5 collective-permute-start.18
  193.1 4.4 %all-to-all-done.3 = bf16[8,16,2048]{2,1,0:T(8,128)(2,1)S(1)} async-done(((bf16[8,16,2048]{2,1,0:T(8,128)(2,1)}), bf16[8,16,2048]{2,1,0:T(8,128)(2,1)S(1)}, u32[]{:S(2)}, u32[]{:S(2)}) %all-to-all-start.3) | async-done | bytes 524320 | tf_op jit(solution)/shard_map/all_to_all | solution.py:23
  197.5 2.7 %collective-permute-done.16 = bf16[256,1024]{1,0:T(8,128)(2,1)} collective-permute-done((bf16[256,1024]{1,0:T(8,128)(2,1)}, bf16[256,1024]{1,0:T(8,128)(2,1)}, u32[]{:S(2)}, u32[]{:S(2)}) %collective-permute-start.16) | collective-permute-done | bytes 524320 | tf_op jit(solution)/shard_map/ppermute | solution.py:15
  200.2 2.1 collective-permute-done.17
  202.3 5.5 %collective-permute-done.18 = bf16[256,1024]{1,0:T(8,128)(2,1)} collective-permute-done((bf16[256,1024]{1,0:T(8,128)(2,1)S(1)}, bf16[256,1024]{1,0:T(8,128)(2,1)}, u32[]{:S(2)}, u32[]{:S(2)}) %collective-permute-start.18) | collective-permute-done | bytes 524320 | tf_op jit(solution)/shard_map/ppermute | solution.py:15
  207.8 2.5 %fusion.69 = bf16[256,1024]{1,0:T(8,128)(2,1)} fusion(bf16[256,1024]{1,0:T(8,128)(2,1)} %collective-permute-done.18, bf16[256,1024]{1,0:T(8,128)(2,1)} %collective-permute-done.17, bf16[256,1024]{1,0:T(8,128)(2,1)} %collective-permute-done.16, bf16[4,256,1024]{2,1,0:T(8,128)(2,1)S(1)} %bitcast.132, s32[]{:T(128)S(6)} %select_n.193), kind=kLoop, calls=%fused_computation.73 | loop fusion | flops 2097152 | bytes 2621444 | tf_op jit(solution)/shard_map/convert_element_type | solution.py:115
  210.3 4.1 %collective-permute-start.13 = (bf16[128,2048]{1,0:T(8,128)(2,1)S(1)}, bf16[128,2048]{1,0:T(8,128)(2,1)S(1)}, u32[]{:S(2)}, u32[]{:S(2)}) collective-permute-start(bf16[128,2048]{1,0:T(8,128)(2,1)S(1)} %bitcast.134), channel_id=1, source_target_pairs={{0,3},{32,33},{1,0},{33,34},{2,1},{34,35},{3,2},{35,32},{4,7},{36,... | collective-permute-start | bytes 1572872 | tf_op jit(solution)/shard_map/ppermute | solution.py:54
  214.4 0.2 broadcast_in_dim.48
  214.7 0.1 bitcast_dynamic-update-slice_fusion.3
  214.8 0.1 collective-permute-start.14
  214.8 1.1 bitcast_dynamic-update-slice_fusion.2
  216.0 9.4 %collective-permute-done.13 = bf16[128,2048]{1,0:T(8,128)(2,1)S(1)} collective-permute-done((bf16[128,2048]{1,0:T(8,128)(2,1)S(1)}, bf16[128,2048]{1,0:T(8,128)(2,1)S(1)}, u32[]{:S(2)}, u32[]{:S(2)}) %collective-permute-start.13) | collective-permute-done | bytes 524320 | tf_op jit(solution)/shard_map/ppermute | solution.py:54
  225.4 0.1 collective-permute-done.14
  225.5 1.3 copy-done.2
  (43 shorter events, 0.4 us)
Async XLA Ops:
  0.6 52.8 %copy-start = (bf16[512,2048]{1,0:T(8,128)(2,1)S(1)}, bf16[512,2048]{1,0:T(8,128)(2,1)}, u32[]{:S(2)}) copy-start(bf16[512,2048]{1,0:T(8,128)(2,1)} %param.5) | copy-start | bytes 6291460
  0.6 49.1 %collective-permute-start.1 = (bf16[8192,128]{1,0:T(8,128)(2,1)}, bf16[8192,128]{1,0:T(8,128)(2,1)}, u32[]{:S(2)}, u32[]{:S(2)}) collective-permute-start(bf16[8192,128]{1,0:T(8,128)(2,1)} %param.8), channel_id=1, source_target_pairs={{0,64},{32,224},{64,128},{96,32},{128,192},{160,96},{192,0},{224,1... | collective-permute-start | bytes 6291464 | tf_op jit(solution)/shard_map/ppermute | solution.py:54
  2.2 50.7 %collective-permute-start.2 = (bf16[8192,128]{1,0:T(8,128)(2,1)}, bf16[8192,128]{1,0:T(8,128)(2,1)}, u32[]{:S(2)}, u32[]{:S(2)}) collective-permute-start(bf16[8192,128]{1,0:T(8,128)(2,1)} %param.8), channel_id=1, source_target_pairs={{0,192},{32,96},{64,0},{96,160},{128,64},{160,224},{192,128},{224,... | collective-permute-start | bytes 6291464 | tf_op jit(solution)/shard_map/ppermute | solution.py:54
  3.1 58.9 %collective-permute-start = (bf16[8192,128]{1,0:T(8,128)(2,1)}, bf16[8192,128]{1,0:T(8,128)(2,1)}, u32[]{:S(2)}, u32[]{:S(2)}) collective-permute-start(bf16[8192,128]{1,0:T(8,128)(2,1)} %param.8), channel_id=1, source_target_pairs={{0,32},{32,0},{1,33},{33,1},{2,34},{34,2},{3,35},{35,3},{4,36},{36... | collective-permute-start | bytes 6291464 | tf_op jit(solution)/shard_map/ppermute | solution.py:15
  52.4 27.1 %collective-permute-start.7 = (bf16[6144,128]{1,0:T(8,128)(2,1)}, bf16[6144,128]{1,0:T(8,128)(2,1)}, u32[]{:S(2)}, u32[]{:S(2)}) collective-permute-start(bf16[6144,128]{1,0:T(8,128)(2,1)} %slice.71), channel_id=1, source_target_pairs={{0,64},{32,224},{64,128},{96,32},{128,192},{160,96},{192,0},{224,1... | collective-permute-start | bytes 4718600 | tf_op jit(solution)/shard_map/ppermute | solution.py:54
  52.9 27.2 %collective-permute-start.4 = (bf16[8192,128]{1,0:T(8,128)(2,1)}, bf16[8192,128]{1,0:T(8,128)(2,1)}, u32[]{:S(2)}, u32[]{:S(2)}) collective-permute-start(bf16[8192,128]{1,0:T(8,128)(2,1)} %collective-permute-done.1), channel_id=1, source_target_pairs={{0,32},{32,0},{1,33},{33,1},{2,34},{34,2},{3,35},{35,3},{4,36},{36... | collective-permute-start | bytes 6291464 | tf_op jit(solution)/shard_map/ppermute | solution.py:15
  52.9 27.2 %collective-permute-start.3 = (bf16[8192,128]{1,0:T(8,128)(2,1)}, bf16[8192,128]{1,0:T(8,128)(2,1)}, u32[]{:S(2)}, u32[]{:S(2)}) collective-permute-start(bf16[8192,128]{1,0:T(8,128)(2,1)} %collective-permute-done.2), channel_id=1, source_target_pairs={{0,32},{32,0},{1,33},{33,1},{2,34},{34,2},{3,35},{35,3},{4,36},{36... | collective-permute-start | bytes 6291464 | tf_op jit(solution)/shard_map/ppermute | solution.py:15
  60.3 19.2 %collective-permute-start.5 = (bf16[2048,128]{1,0:T(8,128)(2,1)S(1)}, bf16[2048,128]{1,0:T(8,128)(2,1)S(1)}, u32[]{:S(2)}, u32[]{:S(2)}) collective-permute-start(bf16[2048,128]{1,0:T(8,128)(2,1)S(1)} %slice.70), channel_id=1, source_target_pairs={{0,64},{32,224},{64,128},{96,32},{128,192},{160,96},{192,0},{224,1... | collective-permute-start | bytes 1572872 | tf_op jit(solution)/shard_map/ppermute | solution.py:54
  61.9 18.2 %slice-start = ((s8[8388608]{0:T(1024)(128)(4,1)}), s8[4194304]{0:T(1024)(128)(4,1)S(1)}, s32[]{:S(2)}) async-start(s8[8388608]{0:T(1024)(128)(4,1)} %bitcast.146), calls=%async_computation.4 | async-start | bytes 8388608
  62.2 17.9 %slice-start.1 = ((s8[8388608]{0:T(1024)(128)(4,1)}), s8[4194304]{0:T(1024)(128)(4,1)S(1)}, s32[]{:S(2)}) async-start(s8[8388608]{0:T(1024)(128)(4,1)} %bitcast.146), calls=%async_computation.5 | async-start | bytes 8388608
  79.6 16.0 %collective-permute-start.6 = (bf16[2048,128]{1,0:T(8,128)(2,1)S(1)}, bf16[2048,128]{1,0:T(8,128)(2,1)S(1)}, u32[]{:S(2)}, u32[]{:S(2)}) collective-permute-start(bf16[2048,128]{1,0:T(8,128)(2,1)S(1)} %collective-permute-done.5), channel_id=1, source_target_pairs={{0,32},{32,0},{1,33},{33,1},{2,34},{34,2},{3,35},{35,3},{4,36},{36... | collective-permute-start | bytes 1572872 | tf_op jit(solution)/shard_map/ppermute | solution.py:15
  79.6 12.2 %collective-permute-start.8 = (bf16[6144,128]{1,0:T(8,128)(2,1)}, bf16[6144,128]{1,0:T(8,128)(2,1)S(1)}, u32[]{:S(2)}, u32[]{:S(2)}) collective-permute-start(bf16[6144,128]{1,0:T(8,128)(2,1)} %collective-permute-done.7), channel_id=1, source_target_pairs={{0,32},{32,0},{1,33},{33,1},{2,34},{34,2},{3,35},{35,3},{4,36},{36... | collective-permute-start | bytes 4718600 | tf_op jit(solution)/shard_map/ppermute | solution.py:15
  96.5 29.9 %copy-start.7 = (f32[512]{0:T(512)S(1)}, f32[512]{0:T(512)}, u32[]{:S(2)}) copy-start(f32[512]{0:T(512)} %param.9) | copy-start | bytes 6148
  108.7 17.5 %all-to-all-start.1 = ((f32[8,5,512]{2,1,0:T(8,128)}), f32[8,5,512]{2,1,0:T(8,128)S(1)}, u32[]{:S(2)}, u32[]{:S(2)}) async-start(f32[8,5,512]{2,1,0:T(8,128)} %broadcast_in_dim.51), calls=%async_computation.1 | async-start | bytes 262144 | tf_op jit(solution)/shard_map/all_to_all | solution.py:23
  127.0 2.8 %copy-start.8 = (bf16[2048,1024]{1,0:T(8,128)(2,1)S(1)}, bf16[2048,1024]{1,0:T(8,128)(2,1)}, u32[]{:S(2)}) copy-start(bf16[2048,1024]{1,0:T(8,128)(2,1)} %param.7) | copy-start | bytes 12582916
  129.8 20.8 %copy-start.4 = (bf16[512,1024]{1,0:T(8,128)(2,1)}, bf16[512,1024]{1,0:T(8,128)(2,1)S(1)}, u32[]{:S(2)}) copy-start(bf16[512,1024]{1,0:T(8,128)(2,1)S(1)} %multiply_convert_fusion) | copy-start | bytes 3145732
  132.3 1.3 copy-start.3
  132.3 2.9 %copy-start.1 = (bf16[512,2048]{1,0:T(8,128)(2,1)S(1)}, bf16[512,2048]{1,0:T(8,128)(2,1)}, u32[]{:S(2)}) copy-start(bf16[512,2048]{1,0:T(8,128)(2,1)} %param.5) | copy-start | bytes 6291460
  134.6 14.6 %collective-permute-start.10 = (bf16[128,2048]{1,0:T(8,128)(2,1)}, bf16[128,2048]{1,0:T(8,128)(2,1)}, u32[]{:S(2)}, u32[]{:S(2)}) collective-permute-start(bf16[128,2048]{1,0:T(8,128)(2,1)} %get-tuple-element.28), channel_id=1, source_target_pairs={{0,1},{32,35},{1,2},{33,32},{2,3},{34,33},{3,0},{35,34},{4,5},{36,... | collective-permute-start | bytes 1572872 | tf_op jit(solution)/shard_map/ppermute | solution.py:54
  136.2 17.0 %collective-permute-start.9 = (bf16[128,2048]{1,0:T(8,128)(2,1)}, bf16[128,2048]{1,0:T(8,128)(2,1)S(1)}, u32[]{:S(2)}, u32[]{:S(2)}) collective-permute-start(bf16[128,2048]{1,0:T(8,128)(2,1)} %get-tuple-element.27), channel_id=1, source_target_pairs={{0,3},{32,33},{1,0},{33,34},{2,1},{34,35},{3,2},{35,32},{4,7},{36,... | collective-permute-start | bytes 1572872 | tf_op jit(solution)/shard_map/ppermute | solution.py:54
  150.5 10.5 %collective-permute-start.11 = (bf16[128,2048]{1,0:T(8,128)(2,1)S(1)}, bf16[128,2048]{1,0:T(8,128)(2,1)S(1)}, u32[]{:S(2)}, u32[]{:S(2)}) collective-permute-start(bf16[128,2048]{1,0:T(8,128)(2,1)S(1)} %fusion.70), channel_id=1, source_target_pairs={{0,1},{32,35},{1,2},{33,32},{2,3},{34,33},{3,0},{35,34},{4,5},{36,... | collective-permute-start | bytes 1572872 | tf_op jit(solution)/shard_map/ppermute | solution.py:54
  153.2 31.1 %collective-permute-start.15 = (bf16[1024,1024]{1,0:T(8,128)(2,1)}, bf16[1024,1024]{1,0:T(8,128)(2,1)}, u32[]{:S(2)}, u32[]{:S(2)}) collective-permute-start(bf16[1024,1024]{1,0:T(8,128)(2,1)} %convolution_convert_fusion.1), channel_id=1, source_target_pairs={{0,32},{32,0},{1,33},{33,1},{2,34},{34,2},{3,35},{35,3},{4,36},{36... | collective-permute-start | bytes 6291464 | tf_op jit(solution)/shard_map/ppermute | solution.py:15
  163.1 21.3 %copy-start.5 = (bf16[512,256]{1,0:T(8,128)(2,1)S(1)}, bf16[512,256]{1,0:T(8,128)(2,1)}, u32[]{:S(2)}) copy-start(bf16[512,256]{1,0:T(8,128)(2,1)} %get-tuple-element.22) | copy-start | bytes 786436
  163.1 21.3 %copy-start.6 = (bf16[512,256]{1,0:T(8,128)(2,1)S(1)}, bf16[512,256]{1,0:T(8,128)(2,1)}, u32[]{:S(2)}) copy-start(bf16[512,256]{1,0:T(8,128)(2,1)} %get-tuple-element.23) | copy-start | bytes 786436
  163.1 16.8 %all-to-all-start.2 = ((bf16[8,16,2048]{2,1,0:T(8,128)(2,1)}), bf16[8,16,2048]{2,1,0:T(8,128)(2,1)S(1)}, u32[]{:S(2)}, u32[]{:S(2)}) async-start(bf16[8,16,2048]{2,1,0:T(8,128)(2,1)} %bitcast.24), calls=%async_computation.2 | async-start | bytes 1048576 | tf_op jit(solution)/shard_map/all_to_all | solution.py:23
  180.8 16.7 %all-to-all-start.3 = ((bf16[8,16,2048]{2,1,0:T(8,128)(2,1)}), bf16[8,16,2048]{2,1,0:T(8,128)(2,1)S(1)}, u32[]{:S(2)}, u32[]{:S(2)}) async-start(bf16[8,16,2048]{2,1,0:T(8,128)(2,1)} %broadcast_in_dim.53), calls=%async_computation.3 | async-start | bytes 1048576 | tf_op jit(solution)/shard_map/all_to_all | solution.py:23
  188.8 11.4 %collective-permute-start.16 = (bf16[256,1024]{1,0:T(8,128)(2,1)}, bf16[256,1024]{1,0:T(8,128)(2,1)}, u32[]{:S(2)}, u32[]{:S(2)}) collective-permute-start(bf16[256,1024]{1,0:T(8,128)(2,1)} %get-tuple-element.16), channel_id=1, source_target_pairs={{0,64},{64,128},{128,192},{192,0},{1,65},{65,129},{129,193},{193,1... | collective-permute-start | bytes 1572872 | tf_op jit(solution)/shard_map/ppermute | solution.py:15
  189.6 12.7 %collective-permute-start.17 = (bf16[256,1024]{1,0:T(8,128)(2,1)}, bf16[256,1024]{1,0:T(8,128)(2,1)}, u32[]{:S(2)}, u32[]{:S(2)}) collective-permute-start(bf16[256,1024]{1,0:T(8,128)(2,1)} %get-tuple-element.18), channel_id=1, source_target_pairs={{0,128},{64,192},{128,0},{192,64},{1,129},{65,193},{129,1},{193,65... | collective-permute-start | bytes 1572872 | tf_op jit(solution)/shard_map/ppermute | solution.py:15
  192.6 15.1 %collective-permute-start.18 = (bf16[256,1024]{1,0:T(8,128)(2,1)S(1)}, bf16[256,1024]{1,0:T(8,128)(2,1)}, u32[]{:S(2)}, u32[]{:S(2)}) collective-permute-start(bf16[256,1024]{1,0:T(8,128)(2,1)S(1)} %get-tuple-element.17), channel_id=1, source_target_pairs={{0,192},{64,0},{128,64},{192,128},{1,193},{65,1},{129,65},{193,129... | collective-permute-start | bytes 1572872 | tf_op jit(solution)/shard_map/ppermute | solution.py:15
  197.5 17.2 %collective-permute-start.12 = (bf16[128,2048]{1,0:T(8,128)(2,1)S(1)}, bf16[128,2048]{1,0:T(8,128)(2,1)}, u32[]{:S(2)}, u32[]{:S(2)}) collective-permute-start(bf16[128,2048]{1,0:T(8,128)(2,1)S(1)} %bitcast.133), channel_id=1, source_target_pairs={{0,1},{32,35},{1,2},{33,32},{2,3},{34,33},{3,0},{35,34},{4,5},{36,... | collective-permute-start | bytes 1572872 | tf_op jit(solution)/shard_map/ppermute | solution.py:54
  210.3 15.0 %collective-permute-start.13 = (bf16[128,2048]{1,0:T(8,128)(2,1)S(1)}, bf16[128,2048]{1,0:T(8,128)(2,1)S(1)}, u32[]{:S(2)}, u32[]{:S(2)}) collective-permute-start(bf16[128,2048]{1,0:T(8,128)(2,1)S(1)} %bitcast.134), channel_id=1, source_target_pairs={{0,3},{32,33},{1,0},{33,34},{2,1},{34,35},{3,2},{35,32},{4,7},{36,... | collective-permute-start | bytes 1572872 | tf_op jit(solution)/shard_map/ppermute | solution.py:54
  214.8 10.7 %collective-permute-start.14 = (bf16[128,2048]{1,0:T(8,128)(2,1)}, bf16[128,2048]{1,0:T(8,128)(2,1)S(1)}, u32[]{:S(2)}, u32[]{:S(2)}) collective-permute-start(bf16[128,2048]{1,0:T(8,128)(2,1)} %collective-permute-done.12), channel_id=1, source_target_pairs={{0,1},{32,35},{1,2},{33,32},{2,3},{34,33},{3,0},{35,34},{4,5},{36,... | collective-permute-start | bytes 1572872 | tf_op jit(solution)/shard_map/ppermute | solution.py:54
  225.5 1.3 copy-start.2

commit v4 on v3

--- a/solution.py
+++ b/solution.py
@@ -134,26 +134,31 @@
     return added(pieces)
 
 
-def summed_ring(pieces, axis):
+def summed_ring(grad_logits, head, axis):
     n, place, core = lax.axis_size(axis), lax.axis_index(axis), lax.axis_index("core")
     back = jnp.where(core == 0, n - 1, 1)
 
-    def piece(step):
+    def product(rows):
+        return dot(rows, head, ((1,), (1,))).astype(jnp.bfloat16)
+
+    def piece(pieces, step):
+        pieces = pieces.reshape(n, -1, pieces.shape[1])
         return lax.dynamic_index_in_dim(pieces, (place + step) % n, 0, keepdims=False)
 
-    far = turned(piece(2), axis, 1)
-    other = turned(piece(back), axis, -1)
-    on = turned(added([far, piece(n - back)]), axis, 1)
-    return added([piece(0), other, on])
-
-
-def summed(part):
-    n, m = lax.axis_size("y"), lax.axis_size("z")
-    rows = summed_ring(part.reshape(n, -1, part.shape[1]), "y")
+    far = turned(product(piece(grad_logits, 2)), axis, 1)
+    pieces = product(grad_logits)
+    other = turned(piece(pieces, back), axis, -1)
+    on = turned(added([far, piece(pieces, n - back)]), axis, 1)
+    return added([piece(pieces, 0), other, on])
+
+
+def summed_product(grad_logits, head):
+    m = lax.axis_size("z")
+    rows = summed_ring(grad_logits, head, "y")
     pieces = exchanged(rows.reshape(m, -1, rows.shape[1]), "z")
     block = added(pieces)
     rows = sent_to_all(block, "z").reshape(rows.shape)
-    return gathered(rows, "y").reshape(part.shape)
+    return gathered(rows, "y").reshape(-1, rows.shape[1])
 
 
 def stage(draft_hidden, teacher_hidden, draft_head, teacher_head, row_weight):
@@ -180,8 +185,7 @@
     draft_prob = jnp.exp(draft_logits - draft_lse[:, None])
     grad_logits = (row_weight[:, None] * (draft_prob - teacher_prob)).astype(jnp.bfloat16)
     grad_head = summed_head(draft_hidden, grad_logits)
-    hidden_part = dot(grad_logits, draft_head, ((1,), (1,))).astype(jnp.bfloat16)
-    grad_hidden = summed(hidden_part)
+    grad_hidden = summed_product(grad_logits, draft_head)
     return (grad_hidden, grad_head, kl_rows)
 
 

time: 229 us -> 226 us (0.987)
  blocking collectives: 8.65 us -> 0 us
  starting transfers between devices: 32.9 us -> 35.8 us
    all_to_all x1 -> x0, blocking collectives: 8.65 us -> none  [exchanged(): return lax.all_to_all(pieces, axis, 0, 0, tiled=True)]
    all_to_all x3 -> x4, starting transfers between devices: 15.6 us -> 18.8 us  [exchanged(): return lax.all_to_all(pieces, axis, 0, 0, tiled=True)]
    all_to_all x3 -> x4, waiting for transfers between devices: 26.7 us -> 29.4 us  [exchanged(): return lax.all_to_all(pieces, axis, 0, 0, tiled=True)]
    dot_general x8 -> x9, matrix products: 38.6 us -> 40.1 us  [dot(): lax.dot_general(a, b, (contract, ((), ())), preferred_element_type=jnp.fl...]
  transfers between devices with their start and end apart: 22 -> 23, of which waited for: 12 -> 13; matrix products, arithmetic and copies ran while one was open for 22% -> 24% of each run, Pallas kernels for 0% -> 0%
where the time goes in v4:
time: 226 us; the launch traced here: 223 us
  waiting for transfers between devices  121 us (54%)
  matrix products  40.1 us (18%)
  starting transfers between devices  35.8 us (16%)
  local copies, waits for them, and re-layouts  14.4 us (6%)
  other arithmetic  10.6 us (5%)
    ppermute x10, waiting for transfers between devices, turned(): return lax.ppermute(piece, axes, pairs)  81.9 us
    dot_general x9, matrix products, dot(): lax.dot_general(a, b, (contract, ((), ())), preferred_element_type=jnp.fl...  40.1 us
    all_to_all x4, waiting for transfers between devices, exchanged(): return lax.all_to_all(pieces, axis, 0, 0, tiled=True)  29.4 us
    all_to_all x4, starting transfers between devices, exchanged(): return lax.all_to_all(pieces, axis, 0, 0, tiled=True)  18.8 us
    ppermute x10, starting transfers between devices, turned(): return lax.ppermute(piece, axes, pairs)  11.6 us
    ppermute x9, waiting for transfers between devices, shifted(): return lax.ppermute(x, axis, [(i, (i + by) % n) for i in range(n)])  10.1 us
    ppermute x9, starting transfers between devices, shifted(): return lax.ppermute(x, axis, [(i, (i + by) % n) for i in range(n)])  5.36 us
  transfers between devices with their start and end apart: 23, of which 13 were waited for; matrix products, arithmetic and copies ran while one was open for 24% of the time, Pallas kernels for 0%

profile of v4, /device:TPU:2, one launch (start us, length us, event | category | flops | bytes accessed | tf_op | source)
XLA Modules:
  0.0 223.4 jit_solution(10071114206299005412)
XLA Ops:
  0.6 1.6 collective-permute-start.1
  2.2 0.8 collective-permute-start.2
  3.1 46.6 %collective-permute-done.1 = bf16[8192,128]{1,0:T(8,128)(2,1)} collective-permute-done((bf16[8192,128]{1,0:T(8,128)(2,1)}, bf16[8192,128]{1,0:T(8,128)(2,1)}, u32[]{:S(2)}, u32[]{:S(2)}) %collective-permute-start.1) | collective-permute-done | bytes 2097184 | tf_op jit(solution)/shard_map/ppermute | solution.py:54
  49.7 2.7 %slice.71 = bf16[6144,128]{1,0:T(8,128)(2,1)} slice(bf16[8192,128]{1,0:T(8,128)(2,1)} %collective-permute-done.1), slice={[0:6144], [0:128]} | slice | bytes 3145728 | tf_op jit(solution)/shard_map/slice | solution.py:73
  52.4 0.4 collective-permute-start.7
  52.9 0.5 collective-permute-start.3
  53.4 5.9 %fusion.102 = (f32[512]{0:T(512)S(1)}, f32[512,1024]{1,0:T(8,128)}) fusion(bf16[512,2048]{1,0:T(8,128)(2,1)S(1)} %copy-done.1, bf16[2048,1024]{1,0:T(8,128)(2,1)} %param.7), kind=kOutput, calls=%fused_computation.143 | convolution fusion | flops 2148007424 | bytes 8390656 | tf_op jit(solution)/shard_map/dot_general | solution.py:19
  59.3 1.1 slice.70
  60.3 1.6 collective-permute-start.5
  61.9 0.2 broadcast_in_dim.49
  62.2 0.0 slice-start.1
  62.2 8.4 %fusion.44 = f32[512,1024]{1,0:T(8,128)S(1)} fusion(f32[512,1024]{1,0:T(8,128)S(1)} %broadcast_in_dim.49, s32[]{:T(128)S(6)} %select_n.164, bf16[512,8192]{1,0:T(8,128)(2,1)} %param.6, bf16[8192,128]{1,0:T(8,128)(2,1)} %collective-permute-done, bf16[8192,128]{1,0:T(8,128)(2,1)} %param.8, pred[]{:T(512)S(6)} %eq.26), kind=kOutput, calls=%fused_computation.49 | convolution fusion | flops 2166358016 | bytes 13107205 | tf_op jit(solution)/shard_map/dot_general | solution.py:19
  70.5 9.0 %collective-permute-done.5 = bf16[2048,128]{1,0:T(8,128)(2,1)S(1)} collective-permute-done((bf16[2048,128]{1,0:T(8,128)(2,1)S(1)}, bf16[2048,128]{1,0:T(8,128)(2,1)S(1)}, u32[]{:S(2)}, u32[]{:S(2)}) %collective-permute-start.5) | collective-permute-done | bytes 524320 | tf_op jit(solution)/shard_map/ppermute | solution.py:54
  79.6 0.5 collective-permute-start.8
  80.1 11.6 %fusion.33 = f32[512,512]{1,0:T(8,128)S(1)} fusion(bf16[512,8192]{1,0:T(8,128)(2,1)S(1)} %bitcast.151, bf16[8192,128]{1,0:T(8,128)(2,1)} %collective-permute-done.4, bf16[8192,128]{1,0:T(8,128)(2,1)} %collective-permute-done.2, bf16[8192,128]{1,0:T(8,128)(2,1)} %collective-permute-done.3, bf16[8192,128]{1,0:T(8,128)(2,1)} %collective-permute-done.1, ...), kind=kOutput, calls=%fused_computation.44 | convolution fusion | flops 4366270464 | bytes 17825792 | tf_op jit(solution)/shard_map/dot_general | solution.py:19
  91.8 0.1 slice_dynamic-update-slice_fusion.1
  91.9 3.8 %fusion.15 = f32[256,512]{0,1:T(8,128)S(1)} fusion(bf16[512,8192]{1,0:T(8,128)(2,1)S(1)} %bitcast.151, bf16[6144,128]{1,0:T(8,128)(2,1)S(1)} %collective-permute-done.8, bf16[6144,128]{1,0:T(8,128)(2,1)} %collective-permute-done.7, pred[]{:T(512)S(6)} %eq.26), kind=kOutput, calls=%fused_computation.16 | convolution fusion | flops 1624768512 | bytes 9961473 | tf_op jit(solution)/shard_map/dot_general | solution.py:19
  95.7 0.7 fusion.40
  96.4 0.2 reduce_max.55
  96.6 2.7 %multiply_reduce_fusion = (f32[512]{0:T(512)S(1)}, f32[512]{0:T(512)S(1)}, f32[512]{0:T(512)S(1)}) fusion(f32[512,1024]{1,0:T(8,128)S(1)} %fusion.40, f32[512,1024]{1,0:T(8,128)} %get-tuple-element.39, f32[512]{0:T(512)S(1)} %reduce_max.55, f32[512]{0:T(512)S(1)} %get-tuple-element.38), kind=kLoop, calls=%fused_computation.37 | loop fusion | flops 3668480 | bytes 4204544 | tf_op jit(solution)/shard_map/reduce_sum | solution.py:176
  99.3 0.6 broadcast_in_dim.50
  100.0 3.3 %all-to-all-start = ((f32[4,5,512]{2,1,0:T(8,128)}), f32[4,5,512]{2,1,0:T(8,128)S(1)}, u32[]{:S(2)}, u32[]{:S(2)}) async-start(f32[4,5,512]{2,1,0:T(8,128)} %broadcast_in_dim.50), calls=%async_computation | async-start | bytes 131072 | tf_op jit(solution)/shard_map/all_to_all | solution.py:23
  103.3 5.5 %all-to-all-done = f32[4,5,512]{2,1,0:T(8,128)S(1)} async-done(((f32[4,5,512]{2,1,0:T(8,128)}), f32[4,5,512]{2,1,0:T(8,128)S(1)}, u32[]{:S(2)}, u32[]{:S(2)}) %all-to-all-start) | async-done | bytes 40992 | tf_op jit(solution)/shard_map/all_to_all | solution.py:23
  109.0 0.7 broadcast_in_dim.51
  109.6 8.4 %all-to-all-start.1 = ((f32[8,5,512]{2,1,0:T(8,128)}), f32[8,5,512]{2,1,0:T(8,128)S(1)}, u32[]{:S(2)}, u32[]{:S(2)}) async-start(f32[8,5,512]{2,1,0:T(8,128)} %broadcast_in_dim.51), calls=%async_computation.1 | async-start | bytes 262144 | tf_op jit(solution)/shard_map/all_to_all | solution.py:23
  118.1 2.8 %constant_dynamic-slice_fusion.7 = (bf16[512,256]{1,0:T(8,128)(2,1)S(1)}, bf16[512,256]{1,0:T(8,128)(2,1)}, bf16[512,256]{1,0:T(8,128)(2,1)}, bf16[512,256]{1,0:...) fusion(bf16[512,2048]{1,0:T(8,128)(2,1)} %param.5, ...), kind=kLoop, calls=%fused_computation.128 | loop fusion | bytes 4194336 | tf_op jit(solution)/shard_map/dynamic_slice | solution.py:126
  120.9 6.3 %all-to-all-done.1 = f32[8,5,512]{2,1,0:T(8,128)S(1)} async-done(((f32[8,5,512]{2,1,0:T(8,128)}), f32[8,5,512]{2,1,0:T(8,128)S(1)}, u32[]{:S(2)}, u32[]{:S(2)}) %all-to-all-start.1) | async-done | bytes 81952 | tf_op jit(solution)/shard_map/all_to_all | solution.py:23
  127.2 0.1 slice_reduce_fusion.3
  127.3 0.6 add_multiply_fusion
  127.9 2.4 %multiply_convert_fusion = bf16[512,1024]{1,0:T(8,128)(2,1)S(1)} fusion(f32[512,1024]{1,0:T(8,128)S(1)} %fusion.40, f32[512,1024]{1,0:T(8,128)} %get-tuple-element.39, f32[512]{0:T(512)S(1)} %get-tuple-element.37, f32[512]{0:T(512)S(1)} %get-tuple-element.15, f32[512]{0:T(512)S(1)} %copy-done.10), kind=kLoop, calls=%fused_computation.36 | loop fusion | flops 2621440 | bytes 5249024 | tf_op jit(solution)/shard_map/convert_element_type | solution.py:186
  130.3 0.4 copy-done
  130.7 1.5 convolution_convert_fusion.1
  132.2 0.6 collective-permute-start.10
  132.9 2.4 %convolution_convert_fusion = bf16[512,2048]{1,0:T(8,128)(2,1)S(1)} fusion(bf16[512,1024]{1,0:T(8,128)(2,1)S(1)} %multiply_convert_fusion, bf16[2048,1024]{1,0:T(8,128)(2,1)S(1)} %copy-done), kind=kOutput, calls=%fused_computation.34 | convolution fusion | flops 2148532224 | bytes 7340032 | tf_op jit(solution)/shard_map/dot_general | solution.py:19
  135.3 0.8 dynamic-slice_bitcast_fusion.3
  136.1 2.7 %collective-permute-start.9 = (bf16[128,2048]{1,0:T(8,128)(2,1)}, bf16[128,2048]{1,0:T(8,128)(2,1)S(1)}, u32[]{:S(2)}, u32[]{:S(2)}) collective-permute-start(bf16[128,2048]{1,0:T(8,128)(2,1)} %dynamic-slice_bitcast_fusion.3), channel_id=1, source_target_pairs={{0,3},{32,33},{1,0},{33,34},{2,1},{34,35},{3,2},{35,32},{4,7},{36,... | collective-permute-start | bytes 1572872 | tf_op jit(solution)/shard_map/ppermute | solution.py:54
  138.8 8.9 %collective-permute-done.10 = bf16[128,2048]{1,0:T(8,128)(2,1)S(1)} collective-permute-done((bf16[128,2048]{1,0:T(8,128)(2,1)S(1)}, bf16[128,2048]{1,0:T(8,128)(2,1)S(1)}, u32[]{:S(2)}, u32[]{:S(2)}) %collective-permute-start.10) | collective-permute-done | bytes 524320 | tf_op jit(solution)/shard_map/ppermute | solution.py:54
  147.7 0.9 fusion.70
  148.6 2.6 %convolution_convert_fusion.2 = bf16[1024,1024]{1,0:T(8,128)(2,1)} fusion(bf16[512,1024]{1,0:T(8,128)(2,1)S(1)} %multiply_convert_fusion, bf16[512,256]{1,0:T(8,128)(2,1)S(1)} %copy-done.8, bf16[512,256]{1,0:T(8,128)(2,1)S(1)} %copy-done.9, bf16[512,256]{1,0:T(8,128)(2,1)S(1)} %copy-done.6, bf16[512,256]{1,0:T(8,128)(2,1)S(1)} %copy-done.7), kind=kOutput, calls=%fused_computation.43 | convolution fusion | flops 1078984704 | bytes 4194304 | tf_op jit(solution)/shard_map/dot_general | solution.py:19
  151.3 7.9 %collective-permute-done.11 = bf16[128,2048]{1,0:T(8,128)(2,1)S(1)} collective-permute-done((bf16[128,2048]{1,0:T(8,128)(2,1)}, bf16[128,2048]{1,0:T(8,128)(2,1)S(1)}, u32[]{:S(2)}, u32[]{:S(2)}) %collective-permute-start.11) | collective-permute-done | bytes 524320 | tf_op jit(solution)/shard_map/ppermute | solution.py:54
  159.2 1.0 fusion.72
  160.2 3.6 %all-to-all-start.2 = ((bf16[8,16,2048]{2,1,0:T(8,128)(2,1)}), bf16[8,16,2048]{2,1,0:T(8,128)(2,1)S(1)}, u32[]{:S(2)}, u32[]{:S(2)}) async-start(bf16[8,16,2048]{2,1,0:T(8,128)(2,1)} %bitcast.25), calls=%async_computation.2 | async-start | bytes 1048576 | tf_op jit(solution)/shard_map/all_to_all | solution.py:23
  163.9 13.2 %all-to-all-done.2 = bf16[8,16,2048]{2,1,0:T(8,128)(2,1)S(1)} async-done(((bf16[8,16,2048]{2,1,0:T(8,128)(2,1)}), bf16[8,16,2048]{2,1,0:T(8,128)(2,1)S(1)}, u32[]{:S(2)}, u32[]{:S(2)}) %all-to-all-start.2) | async-done | bytes 524320 | tf_op jit(solution)/shard_map/all_to_all | solution.py:23
  177.1 0.1 fusion.76
  177.1 0.8 broadcast_in_dim.53
  178.0 3.5 %all-to-all-start.3 = ((bf16[8,16,2048]{2,1,0:T(8,128)(2,1)}), bf16[8,16,2048]{2,1,0:T(8,128)(2,1)S(1)}, u32[]{:S(2)}, u32[]{:S(2)}) async-start(bf16[8,16,2048]{2,1,0:T(8,128)(2,1)} %broadcast_in_dim.53), calls=%async_computation.3 | async-start | bytes 1048576 | tf_op jit(solution)/shard_map/all_to_all | solution.py:23
  181.5 3.3 %add_convert_fusion = bf16[1024,1024]{1,0:T(8,128)(2,1)S(1)} fusion(bf16[1024,1024]{1,0:T(8,128)(2,1)} %collective-permute-done.15, bf16[512,1024]{1,0:T(8,128)(2,1)} %copy-done.3, bf16[512,256]{1,0:T(8,128)(2,1)S(1)} %copy-done.4, bf16[512,256]{1,0:T(8,128)(2,1)S(1)} %copy-done.5, bf16[512,256]{1,0:T(8,128)(2,1)} %get-tuple-element.24, ...), kind=kOutput, calls=%fused_computation.25 | convolution fusion | flops 1081081856 | bytes 6291456 | tf_op jit(solution)/shard_map/dot_general | solution.py:19
  184.8 1.1 dynamic-slice_bitcast_fusion.2
  186.0 0.8 collective-permute-start.16
  186.7 3.1 %collective-permute-start.17 = (bf16[256,1024]{1,0:T(8,128)(2,1)}, bf16[256,1024]{1,0:T(8,128)(2,1)}, u32[]{:S(2)}, u32[]{:S(2)}) collective-permute-start(bf16[256,1024]{1,0:T(8,128)(2,1)} %get-tuple-element.18), channel_id=1, source_target_pairs={{0,128},{64,192},{128,0},{192,64},{1,129},{65,193},{129,1},{193,65... | collective-permute-start | bytes 1572872 | tf_op jit(solution)/shard_map/ppermute | solution.py:15
  189.8 0.5 collective-permute-start.18
  190.3 4.4 %all-to-all-done.3 = bf16[8,16,2048]{2,1,0:T(8,128)(2,1)S(1)} async-done(((bf16[8,16,2048]{2,1,0:T(8,128)(2,1)}), bf16[8,16,2048]{2,1,0:T(8,128)(2,1)S(1)}, u32[]{:S(2)}, u32[]{:S(2)}) %all-to-all-start.3) | async-done | bytes 524320 | tf_op jit(solution)/shard_map/all_to_all | solution.py:23
  194.7 2.5 %collective-permute-done.16 = bf16[256,1024]{1,0:T(8,128)(2,1)} collective-permute-done((bf16[256,1024]{1,0:T(8,128)(2,1)}, bf16[256,1024]{1,0:T(8,128)(2,1)}, u32[]{:S(2)}, u32[]{:S(2)}) %collective-permute-start.16) | collective-permute-done | bytes 524320 | tf_op jit(solution)/shard_map/ppermute | solution.py:15
  197.2 2.1 collective-permute-done.17
  199.3 5.5 %collective-permute-done.18 = bf16[256,1024]{1,0:T(8,128)(2,1)} collective-permute-done((bf16[256,1024]{1,0:T(8,128)(2,1)S(1)}, bf16[256,1024]{1,0:T(8,128)(2,1)}, u32[]{:S(2)}, u32[]{:S(2)}) %collective-permute-start.18) | collective-permute-done | bytes 524320 | tf_op jit(solution)/shard_map/ppermute | solution.py:15
  204.8 2.5 %fusion.69 = bf16[256,1024]{1,0:T(8,128)(2,1)} fusion(bf16[256,1024]{1,0:T(8,128)(2,1)} %collective-permute-done.18, bf16[256,1024]{1,0:T(8,128)(2,1)} %collective-permute-done.17, bf16[256,1024]{1,0:T(8,128)(2,1)} %collective-permute-done.16, bf16[4,256,1024]{2,1,0:T(8,128)(2,1)S(1)} %bitcast.132, s32[]{:T(128)S(6)} %select_n.194), kind=kLoop, calls=%fused_computation.74 | loop fusion | flops 2097152 | bytes 2621444 | tf_op jit(solution)/shard_map/convert_element_type | solution.py:115
  207.3 3.8 %collective-permute-start.13 = (bf16[128,2048]{1,0:T(8,128)(2,1)S(1)}, bf16[128,2048]{1,0:T(8,128)(2,1)S(1)}, u32[]{:S(2)}, u32[]{:S(2)}) collective-permute-start(bf16[128,2048]{1,0:T(8,128)(2,1)S(1)} %bitcast.134), channel_id=1, source_target_pairs={{0,3},{32,33},{1,0},{33,34},{2,1},{34,35},{3,2},{35,32},{4,7},{36,... | collective-permute-start | bytes 1572872 | tf_op jit(solution)/shard_map/ppermute | solution.py:54
  211.1 0.2 broadcast_in_dim.48
  211.3 0.1 bitcast_dynamic-update-slice_fusion.3
  211.4 0.1 collective-permute-start.14
  211.5 1.1 bitcast_dynamic-update-slice_fusion.2
  212.6 9.0 %collective-permute-done.13 = bf16[128,2048]{1,0:T(8,128)(2,1)S(1)} collective-permute-done((bf16[128,2048]{1,0:T(8,128)(2,1)S(1)}, bf16[128,2048]{1,0:T(8,128)(2,1)S(1)}, u32[]{:S(2)}, u32[]{:S(2)}) %collective-permute-start.13) | collective-permute-done | bytes 524320 | tf_op jit(solution)/shard_map/ppermute | solution.py:54
  221.7 0.4 collective-permute-done.14
  222.1 1.3 copy-done.2
  (49 shorter events, 0.4 us)
Async XLA Ops:
  0.6 52.8 %copy-start.1 = (bf16[512,2048]{1,0:T(8,128)(2,1)S(1)}, bf16[512,2048]{1,0:T(8,128)(2,1)}, u32[]{:S(2)}) copy-start(bf16[512,2048]{1,0:T(8,128)(2,1)} %param.5) | copy-start | bytes 6291460
  0.6 49.1 %collective-permute-start.1 = (bf16[8192,128]{1,0:T(8,128)(2,1)}, bf16[8192,128]{1,0:T(8,128)(2,1)}, u32[]{:S(2)}, u32[]{:S(2)}) collective-permute-start(bf16[8192,128]{1,0:T(8,128)(2,1)} %param.8), channel_id=1, source_target_pairs={{0,64},{32,224},{64,128},{96,32},{128,192},{160,96},{192,0},{224,1... | collective-permute-start | bytes 6291464 | tf_op jit(solution)/shard_map/ppermute | solution.py:54
  2.2 50.7 %collective-permute-start.2 = (bf16[8192,128]{1,0:T(8,128)(2,1)}, bf16[8192,128]{1,0:T(8,128)(2,1)}, u32[]{:S(2)}, u32[]{:S(2)}) collective-permute-start(bf16[8192,128]{1,0:T(8,128)(2,1)} %param.8), channel_id=1, source_target_pairs={{0,192},{32,96},{64,0},{96,160},{128,64},{160,224},{192,128},{224,... | collective-permute-start | bytes 6291464 | tf_op jit(solution)/shard_map/ppermute | solution.py:54
  3.1 58.8 %collective-permute-start = (bf16[8192,128]{1,0:T(8,128)(2,1)}, bf16[8192,128]{1,0:T(8,128)(2,1)}, u32[]{:S(2)}, u32[]{:S(2)}) collective-permute-start(bf16[8192,128]{1,0:T(8,128)(2,1)} %param.8), channel_id=1, source_target_pairs={{0,32},{32,0},{1,33},{33,1},{2,34},{34,2},{3,35},{35,3},{4,36},{36... | collective-permute-start | bytes 6291464 | tf_op jit(solution)/shard_map/ppermute | solution.py:15
  52.4 27.1 %collective-permute-start.7 = (bf16[6144,128]{1,0:T(8,128)(2,1)}, bf16[6144,128]{1,0:T(8,128)(2,1)}, u32[]{:S(2)}, u32[]{:S(2)}) collective-permute-start(bf16[6144,128]{1,0:T(8,128)(2,1)} %slice.71), channel_id=1, source_target_pairs={{0,64},{32,224},{64,128},{96,32},{128,192},{160,96},{192,0},{224,1... | collective-permute-start | bytes 4718600 | tf_op jit(solution)/shard_map/ppermute | solution.py:54
  52.9 27.2 %collective-permute-start.4 = (bf16[8192,128]{1,0:T(8,128)(2,1)}, bf16[8192,128]{1,0:T(8,128)(2,1)}, u32[]{:S(2)}, u32[]{:S(2)}) collective-permute-start(bf16[8192,128]{1,0:T(8,128)(2,1)} %collective-permute-done.1), channel_id=1, source_target_pairs={{0,32},{32,0},{1,33},{33,1},{2,34},{34,2},{3,35},{35,3},{4,36},{36... | collective-permute-start | bytes 6291464 | tf_op jit(solution)/shard_map/ppermute | solution.py:15
  52.9 27.2 %collective-permute-start.3 = (bf16[8192,128]{1,0:T(8,128)(2,1)}, bf16[8192,128]{1,0:T(8,128)(2,1)}, u32[]{:S(2)}, u32[]{:S(2)}) collective-permute-start(bf16[8192,128]{1,0:T(8,128)(2,1)} %collective-permute-done.2), channel_id=1, source_target_pairs={{0,32},{32,0},{1,33},{33,1},{2,34},{34,2},{3,35},{35,3},{4,36},{36... | collective-permute-start | bytes 6291464 | tf_op jit(solution)/shard_map/ppermute | solution.py:15
  60.3 19.2 %collective-permute-start.5 = (bf16[2048,128]{1,0:T(8,128)(2,1)S(1)}, bf16[2048,128]{1,0:T(8,128)(2,1)S(1)}, u32[]{:S(2)}, u32[]{:S(2)}) collective-permute-start(bf16[2048,128]{1,0:T(8,128)(2,1)S(1)} %slice.70), channel_id=1, source_target_pairs={{0,64},{32,224},{64,128},{96,32},{128,192},{160,96},{192,0},{224,1... | collective-permute-start | bytes 1572872 | tf_op jit(solution)/shard_map/ppermute | solution.py:54
  61.9 18.2 %slice-start = ((s8[8388608]{0:T(1024)(128)(4,1)}), s8[4194304]{0:T(1024)(128)(4,1)S(1)}, s32[]{:S(2)}) async-start(s8[8388608]{0:T(1024)(128)(4,1)} %bitcast.150), calls=%async_computation.4 | async-start | bytes 8388608
  62.2 17.9 %slice-start.1 = ((s8[8388608]{0:T(1024)(128)(4,1)}), s8[4194304]{0:T(1024)(128)(4,1)S(1)}, s32[]{:S(2)}) async-start(s8[8388608]{0:T(1024)(128)(4,1)} %bitcast.150), calls=%async_computation.5 | async-start | bytes 8388608
  79.6 16.1 %collective-permute-start.6 = (bf16[2048,128]{1,0:T(8,128)(2,1)S(1)}, bf16[2048,128]{1,0:T(8,128)(2,1)S(1)}, u32[]{:S(2)}, u32[]{:S(2)}) collective-permute-start(bf16[2048,128]{1,0:T(8,128)(2,1)S(1)} %collective-permute-done.5), channel_id=1, source_target_pairs={{0,32},{32,0},{1,33},{33,1},{2,34},{34,2},{3,35},{35,3},{4,36},{36... | collective-permute-start | bytes 1572872 | tf_op jit(solution)/shard_map/ppermute | solution.py:15
  79.6 12.3 %collective-permute-start.8 = (bf16[6144,128]{1,0:T(8,128)(2,1)}, bf16[6144,128]{1,0:T(8,128)(2,1)S(1)}, u32[]{:S(2)}, u32[]{:S(2)}) collective-permute-start(bf16[6144,128]{1,0:T(8,128)(2,1)} %collective-permute-done.7), channel_id=1, source_target_pairs={{0,32},{32,0},{1,33},{33,1},{2,34},{34,2},{3,35},{35,3},{4,36},{36... | collective-permute-start | bytes 4718600 | tf_op jit(solution)/shard_map/ppermute | solution.py:15
  100.0 8.9 %all-to-all-start = ((f32[4,5,512]{2,1,0:T(8,128)}), f32[4,5,512]{2,1,0:T(8,128)S(1)}, u32[]{:S(2)}, u32[]{:S(2)}) async-start(f32[4,5,512]{2,1,0:T(8,128)} %broadcast_in_dim.50), calls=%async_computation | async-start | bytes 131072 | tf_op jit(solution)/shard_map/all_to_all | solution.py:23
  109.6 17.5 %all-to-all-start.1 = ((f32[8,5,512]{2,1,0:T(8,128)}), f32[8,5,512]{2,1,0:T(8,128)S(1)}, u32[]{:S(2)}, u32[]{:S(2)}) async-start(f32[8,5,512]{2,1,0:T(8,128)} %broadcast_in_dim.51), calls=%async_computation.1 | async-start | bytes 262144 | tf_op jit(solution)/shard_map/all_to_all | solution.py:23
  118.1 9.2 %copy-start.10 = (f32[512]{0:T(512)S(1)}, f32[512]{0:T(512)}, u32[]{:S(2)}) copy-start(f32[512]{0:T(512)} %param.9) | copy-start | bytes 6148
  127.9 2.8 %copy-start = (bf16[2048,1024]{1,0:T(8,128)(2,1)S(1)}, bf16[2048,1024]{1,0:T(8,128)(2,1)}, u32[]{:S(2)}) copy-start(bf16[2048,1024]{1,0:T(8,128)(2,1)} %param.7) | copy-start | bytes 12582916
  130.3 18.3 %copy-start.3 = (bf16[512,1024]{1,0:T(8,128)(2,1)}, bf16[512,1024]{1,0:T(8,128)(2,1)S(1)}, u32[]{:S(2)}) copy-start(bf16[512,1024]{1,0:T(8,128)(2,1)S(1)} %multiply_convert_fusion) | copy-start | bytes 3145732
  132.2 15.4 %collective-permute-start.10 = (bf16[128,2048]{1,0:T(8,128)(2,1)S(1)}, bf16[128,2048]{1,0:T(8,128)(2,1)S(1)}, u32[]{:S(2)}, u32[]{:S(2)}) collective-permute-start(bf16[128,2048]{1,0:T(8,128)(2,1)S(1)} %convolution_convert_fusion.1), channel_id=1, source_target_pairs={{0,1},{32,35},{1,2},{33,32},{2,3},{34,33},{3,0},{35,34},{4,5},{36,... | collective-permute-start | bytes 1572872 | tf_op jit(solution)/shard_map/ppermute | solution.py:54
  135.3 13.3 %copy-start.6 = (bf16[512,256]{1,0:T(8,128)(2,1)S(1)}, bf16[512,256]{1,0:T(8,128)(2,1)}, u32[]{:S(2)}) copy-start(bf16[512,256]{1,0:T(8,128)(2,1)} %get-tuple-element.20) | copy-start | bytes 786436
  135.3 13.3 %copy-start.7 = (bf16[512,256]{1,0:T(8,128)(2,1)S(1)}, bf16[512,256]{1,0:T(8,128)(2,1)}, u32[]{:S(2)}) copy-start(bf16[512,256]{1,0:T(8,128)(2,1)} %get-tuple-element.21) | copy-start | bytes 786436
  135.3 13.3 %copy-start.8 = (bf16[512,256]{1,0:T(8,128)(2,1)S(1)}, bf16[512,256]{1,0:T(8,128)(2,1)}, u32[]{:S(2)}) copy-start(bf16[512,256]{1,0:T(8,128)(2,1)} %get-tuple-element.25) | copy-start | bytes 786436
  135.3 13.3 %copy-start.9 = (bf16[512,256]{1,0:T(8,128)(2,1)S(1)}, bf16[512,256]{1,0:T(8,128)(2,1)}, u32[]{:S(2)}) copy-start(bf16[512,256]{1,0:T(8,128)(2,1)} %get-tuple-element.26) | copy-start | bytes 786436
  136.1 15.1 %collective-permute-start.9 = (bf16[128,2048]{1,0:T(8,128)(2,1)}, bf16[128,2048]{1,0:T(8,128)(2,1)S(1)}, u32[]{:S(2)}, u32[]{:S(2)}) collective-permute-start(bf16[128,2048]{1,0:T(8,128)(2,1)} %dynamic-slice_bitcast_fusion.3), channel_id=1, source_target_pairs={{0,3},{32,33},{1,0},{33,34},{2,1},{34,35},{3,2},{35,32},{4,7},{36,... | collective-permute-start | bytes 1572872 | tf_op jit(solution)/shard_map/ppermute | solution.py:54
  148.6 10.6 %collective-permute-start.11 = (bf16[128,2048]{1,0:T(8,128)(2,1)}, bf16[128,2048]{1,0:T(8,128)(2,1)S(1)}, u32[]{:S(2)}, u32[]{:S(2)}) collective-permute-start(bf16[128,2048]{1,0:T(8,128)(2,1)} %fusion.70), channel_id=1, source_target_pairs={{0,1},{32,35},{1,2},{33,32},{2,3},{34,33},{3,0},{35,34},{4,5},{36,... | collective-permute-start | bytes 1572872 | tf_op jit(solution)/shard_map/ppermute | solution.py:54
  151.2 30.3 %collective-permute-start.15 = (bf16[1024,1024]{1,0:T(8,128)(2,1)}, bf16[1024,1024]{1,0:T(8,128)(2,1)}, u32[]{:S(2)}, u32[]{:S(2)}) collective-permute-start(bf16[1024,1024]{1,0:T(8,128)(2,1)} %convolution_convert_fusion.2), channel_id=1, source_target_pairs={{0,32},{32,0},{1,33},{33,1},{2,34},{34,2},{3,35},{35,3},{4,36},{36... | collective-permute-start | bytes 6291464 | tf_op jit(solution)/shard_map/ppermute | solution.py:15
  160.2 21.3 %copy-start.4 = (bf16[512,256]{1,0:T(8,128)(2,1)S(1)}, bf16[512,256]{1,0:T(8,128)(2,1)}, u32[]{:S(2)}) copy-start(bf16[512,256]{1,0:T(8,128)(2,1)} %get-tuple-element.22) | copy-start | bytes 786436
  160.2 21.3 %copy-start.5 = (bf16[512,256]{1,0:T(8,128)(2,1)S(1)}, bf16[512,256]{1,0:T(8,128)(2,1)}, u32[]{:S(2)}) copy-start(bf16[512,256]{1,0:T(8,128)(2,1)} %get-tuple-element.23) | copy-start | bytes 786436
  160.2 16.8 %all-to-all-start.2 = ((bf16[8,16,2048]{2,1,0:T(8,128)(2,1)}), bf16[8,16,2048]{2,1,0:T(8,128)(2,1)S(1)}, u32[]{:S(2)}, u32[]{:S(2)}) async-start(bf16[8,16,2048]{2,1,0:T(8,128)(2,1)} %bitcast.25), calls=%async_computation.2 | async-start | bytes 1048576 | tf_op jit(solution)/shard_map/all_to_all | solution.py:23
  178.0 16.7 %all-to-all-start.3 = ((bf16[8,16,2048]{2,1,0:T(8,128)(2,1)}), bf16[8,16,2048]{2,1,0:T(8,128)(2,1)S(1)}, u32[]{:S(2)}, u32[]{:S(2)}) async-start(bf16[8,16,2048]{2,1,0:T(8,128)(2,1)} %broadcast_in_dim.53), calls=%async_computation.3 | async-start | bytes 1048576 | tf_op jit(solution)/shard_map/all_to_all | solution.py:23
  186.0 11.2 %collective-permute-start.16 = (bf16[256,1024]{1,0:T(8,128)(2,1)}, bf16[256,1024]{1,0:T(8,128)(2,1)}, u32[]{:S(2)}, u32[]{:S(2)}) collective-permute-start(bf16[256,1024]{1,0:T(8,128)(2,1)} %get-tuple-element.16), channel_id=1, source_target_pairs={{0,64},{64,128},{128,192},{192,0},{1,65},{65,129},{129,193},{193,1... | collective-permute-start | bytes 1572872 | tf_op jit(solution)/shard_map/ppermute | solution.py:15
  186.7 12.5 %collective-permute-start.17 = (bf16[256,1024]{1,0:T(8,128)(2,1)}, bf16[256,1024]{1,0:T(8,128)(2,1)}, u32[]{:S(2)}, u32[]{:S(2)}) collective-permute-start(bf16[256,1024]{1,0:T(8,128)(2,1)} %get-tuple-element.18), channel_id=1, source_target_pairs={{0,128},{64,192},{128,0},{192,64},{1,129},{65,193},{129,1},{193,65... | collective-permute-start | bytes 1572872 | tf_op jit(solution)/shard_map/ppermute | solution.py:15
  189.8 14.9 %collective-permute-start.18 = (bf16[256,1024]{1,0:T(8,128)(2,1)S(1)}, bf16[256,1024]{1,0:T(8,128)(2,1)}, u32[]{:S(2)}, u32[]{:S(2)}) collective-permute-start(bf16[256,1024]{1,0:T(8,128)(2,1)S(1)} %get-tuple-element.17), channel_id=1, source_target_pairs={{0,192},{64,0},{128,64},{192,128},{1,193},{65,1},{129,65},{193,129... | collective-permute-start | bytes 1572872 | tf_op jit(solution)/shard_map/ppermute | solution.py:15
  194.7 16.7 %collective-permute-start.12 = (bf16[128,2048]{1,0:T(8,128)(2,1)S(1)}, bf16[128,2048]{1,0:T(8,128)(2,1)}, u32[]{:S(2)}, u32[]{:S(2)}) collective-permute-start(bf16[128,2048]{1,0:T(8,128)(2,1)S(1)} %bitcast.133), channel_id=1, source_target_pairs={{0,1},{32,35},{1,2},{33,32},{2,3},{34,33},{3,0},{35,34},{4,5},{36,... | collective-permute-start | bytes 1572872 | tf_op jit(solution)/shard_map/ppermute | solution.py:54
  207.3 14.3 %collective-permute-start.13 = (bf16[128,2048]{1,0:T(8,128)(2,1)S(1)}, bf16[128,2048]{1,0:T(8,128)(2,1)S(1)}, u32[]{:S(2)}, u32[]{:S(2)}) collective-permute-start(bf16[128,2048]{1,0:T(8,128)(2,1)S(1)} %bitcast.134), channel_id=1, source_target_pairs={{0,3},{32,33},{1,0},{33,34},{2,1},{34,35},{3,2},{35,32},{4,7},{36,... | collective-permute-start | bytes 1572872 | tf_op jit(solution)/shard_map/ppermute | solution.py:54
  211.4 10.7 %collective-permute-start.14 = (bf16[128,2048]{1,0:T(8,128)(2,1)}, bf16[128,2048]{1,0:T(8,128)(2,1)S(1)}, u32[]{:S(2)}, u32[]{:S(2)}) collective-permute-start(bf16[128,2048]{1,0:T(8,128)(2,1)} %collective-permute-done.12), channel_id=1, source_target_pairs={{0,1},{32,35},{1,2},{33,32},{2,3},{34,33},{3,0},{35,34},{4,5},{36,... | collective-permute-start | bytes 1572872 | tf_op jit(solution)/shard_map/ppermute | solution.py:54
  222.1 1.3 copy-start.2
